TPU v7x, 32 devices: a whole 2x2x4 slice. The times are simulated.
32 devices in a mesh: grp: 2 (over y), inp: 4 (over z), tm: 2 (over x), pol: 2 (over core).
Axes of the slice: x: 2, y: 2, z: 4, core: 2. Of those that a mesh axis runs over, the one named last changes fastest.
Arguments:
- samples: bfloat16 [512, 64, 4096], P(('grp', 'inp'), ('tm', 'pol')), parts along dimension 0, may hold values from -6 to 6
- coefficients: float32 [16, 4096], replicated, may hold values from -1.5 to 1.5
Outputs:
- visibilities: float32 [4096, 256, 256], P(('grp', 'inp', 'tm', 'pol')), parts along dimension 0
There are 2 independent parts, one for each index of `grp`. A program takes and returns all parts, laid end to end along the dimension named above; an argument that names none is the same for every part. Nothing has to cross between parts.
All inputs are finite; a program needn't handle non-finite values.
Results may differ from a plain program's by a relative error of at most 0.0034.
Values may be sent and summed in bfloat16 or wider, within the bound.
No kernel may reach another device: no remote copies, remote signals or barrier semaphores. Data moves between devices by JAX's collectives and lax.ppermute only.
A program may use at most 256 MiB of HBM per device.

v0:
```python
import math

import jax
import jax.numpy as jnp
from jax import lax
from jax.sharding import PartitionSpec as P


def from_behind(block, axis, distance):
    devices = range(lax.axis_size(axis))
    route = [(i - distance, i) for i in devices if i - distance in devices]
    return lax.ppermute(block, axis, route)


def correlate(real_part, imag_part, total_frames):
    joined = jnp.concatenate([real_part, imag_part], axis=2)
    turned = jnp.concatenate([imag_part, -real_part], axis=2)
    stacked = jnp.concatenate([joined, turned], axis=1)
    product = jnp.einsum("cif,cjf->cij", stacked, joined, preferred_element_type=jnp.float32)
    width = real_part.shape[1]
    row_index = lax.broadcasted_iota(jnp.int32, (width, width), 0)
    col_index = lax.broadcasted_iota(jnp.int32, (width, width), 1)
    packed = jnp.where(row_index <= col_index, product[:, :width], product[:, width:])
    return packed * (1.0 / total_frames)


def filter_frames(block, coefficients, taps):
    frame_count = block.shape[1] - taps + 1
    total = jnp.zeros((block.shape[0], frame_count, block.shape[2]), jnp.float32)
    for tap_index in range(taps):
        total = total + coefficients[tap_index] * block[
            :, tap_index : tap_index + frame_count
        ].astype(jnp.float32)
    return total


def angles(first_idx, second_idx, period):
    product = first_idx[:, None] * second_idx[None, :] % period
    return product.astype(jnp.float32) * (2.0 * math.pi / period)


def transform(filtered):
    row_total, length = filtered.shape
    inner_len = 2 ** ((length.bit_length() - 1) // 2)
    outer_len = length // inner_len
    blocks = filtered.reshape(row_total, inner_len, outer_len)
    inner_idx = jnp.arange(inner_len, dtype=jnp.int32)
    outer_idx = jnp.arange(outer_len, dtype=jnp.int32)
    half_idx = jnp.arange(outer_len // 2, dtype=jnp.int32)
    angle_one = angles(inner_idx, inner_idx, inner_len)
    table_one = jnp.concatenate([jnp.cos(angle_one), -jnp.sin(angle_one)], axis=1)
    section_one = jnp.einsum("rab,ak->rbk", blocks, table_one, precision=lax.Precision.HIGHEST)
    first_re = section_one[..., :inner_len]
    first_im = section_one[..., inner_len:]
    angle_twist = angles(outer_idx, inner_idx, length)
    twist_cos = jnp.cos(angle_twist)
    twist_sin = jnp.sin(angle_twist)
    turned_re = first_re * twist_cos + first_im * twist_sin
    turned_im = first_im * twist_cos - first_re * twist_sin
    angle_two = angles(outer_idx, half_idx, outer_len)
    table_cos = jnp.cos(angle_two)
    table_sin = jnp.sin(angle_two)
    highest = lax.Precision.HIGHEST
    out_re = jnp.einsum("rbk,bq->qkr", turned_re, table_cos, precision=highest) + jnp.einsum(
        "rbk,bq->qkr", turned_im, table_sin, precision=highest
    )
    out_im = jnp.einsum("rbk,bq->qkr", turned_im, table_cos, precision=highest) - jnp.einsum(
        "rbk,bq->qkr", turned_re, table_sin, precision=highest
    )
    scale_factor = 1.0 / math.sqrt(length)
    return jnp.stack([out_re, out_im]).reshape(2, length // 2, row_total) * scale_factor


def per_device(samples, coefficients):
    in_dev, frame_count, length = samples.shape
    taps = coefficients.shape[0]
    channels = length // 2
    history = from_behind(samples[:, frame_count - taps + 1 :, :], ("tm", "pol"), 1)
    extended = jnp.concatenate([history, samples], axis=1)
    group_size = math.gcd(in_dev, 4)
    spectra_buf = jnp.zeros((2, channels, in_dev, frame_count), jnp.bfloat16)

    def one_group(group_index, buffer_now):
        block = lax.dynamic_slice_in_dim(extended, group_index * group_size, group_size, 0)
        filtered = filter_frames(block, coefficients, taps).reshape(
            group_size * frame_count, length
        )
        spectra_grp = (
            transform(filtered).reshape(2, channels, group_size, frame_count).astype(jnp.bfloat16)
        )
        return lax.dynamic_update_slice_in_dim(buffer_now, spectra_grp, group_index * group_size, 2)

    local_spec = lax.fori_loop(0, in_dev // group_size, one_group, spectra_buf)
    n_inputs = lax.axis_size("inp")
    n_blocks = lax.axis_size("tm")
    n_halves = lax.axis_size("pol")
    total_frames = frame_count * n_blocks * n_halves
    arrived = lax.all_to_all(
        local_spec[None], ("inp", "tm", "pol"), split_axis=2, concat_axis=0, tiled=True
    )
    width = arrived.shape[2]
    arrived = arrived.reshape(n_inputs, n_blocks * n_halves, 2, width, in_dev, frame_count)
    arrived = jnp.transpose(arrived, (2, 3, 0, 4, 1, 5)).reshape(
        2, width, n_inputs * in_dev, n_blocks * n_halves * frame_count
    )
    return correlate(arrived[0], arrived[1], total_frames)


def solution(mesh):
    placed = (P(("grp", "inp"), ("tm", "pol"), None), P())
    return jax.shard_map(
        per_device,
        mesh=mesh,
        in_specs=placed,
        out_specs=P(("grp", "inp", "tm", "pol"), None, None),
        check_vma=False,
    )
```

profile of v0, /device:TPU:15, one launch (start us, length us, event | category | flops | bytes accessed | tf_op | source)
XLA Modules:
  0.0 989.8 jit_solution(8066666141013795568)
XLA Ops:
  0.0 10.5 %slice.391 = bf16[64,15,4096]{2,1,0:T(8,128)(2,1)} slice(bf16[64,16,4096]{2,1,0:T(8,128)(2,1)} %param.4), slice={[0:64], [1:16], [0:4096]} | slice | bytes 15728640 | tf_op jit(solution)/shard_map/slice | solution.py:78
  10.5 11.0 %copy.61 = bf16[64,15,4096]{2,0,1:T(8,128)(2,1)} copy(bf16[64,15,4096]{2,1,0:T(8,128)(2,1)} %slice.391) | data formatting | bytes 15728640
  23.0 13.3 %collective-permute-done = bf16[64,15,4096]{2,0,1:T(8,128)(2,1)} collective-permute-done((bf16[64,15,4096]{2,0,1:T(8,128)(2,1)}, bf16[64,15,4096]{2,0,1:T(8,128)(2,1)}, u32[]{:S(2)}, u32[]{:S(2)}) %collective-permute-start) | collective-permute-done | bytes 7864352 | tf_op jit(solution)/shard_map/ppermute | solution.py:12
  36.3 10.8 %copy.45 = bf16[64,15,4096]{2,1,0:T(8,128)(2,1)} copy(bf16[64,15,4096]{2,0,1:T(8,128)(2,1)} %collective-permute-done) | data formatting | bytes 15728640 | tf_op jit(solution)/shard_map/ppermute | solution.py:12
  47.1 14.9 %pad_maximum_fusion = bf16[64,31,4096]{2,1,0:T(8,128)(2,1)} fusion(bf16[64,16,4096]{2,1,0:T(8,128)(2,1)} %param.4, bf16[64,15,4096]{2,1,0:T(8,128)(2,1)} %copy.45), kind=kLoop, calls=%fused_computation.71 | loop fusion | flops 32505856 | bytes 32505856 | tf_op jit(solution)/shard_map/concatenate | solution.py:79
  62.1 4.3 broadcast_in_dim.31
  66.4 447.5 %while.16 = (s32[]{:T(128)}, bf16[2,2048,64,16]{1,3,2,0:T(8,128)(2,1)}, f32[16,4096]{1,0:T(8,128)S(1)}, bf16[64,31,4096]{2,1,0:T(8,128)(2,1)}, s32[]{:T(128)}, /...) while((s32[]{:T(128)}, ...), condition=%wide.region_1.2_spmd, body=%wide.region_0.1_spmd.sunk | while | flops 822063104 | bytes 40468980 | solution.py:93
  67.4 10.2 %multiply_add_fusion.9 = f32[4,16,4096]{2,1,0:T(8,128)S(1)} fusion(bf16[64,31,4096]{2,1,0:T(8,128)(2,1)} %get-tuple-element.280, s32[]{:T(128)S(6)} %select_n.151, s32[]{:T(128)S(6)} %add.431, s32[]{:T(128)S(6)} %add.432, s32[]{:T(128)S(6)} %add.433, s32[]{:T(128)S(6)} %add.434, s32[]{:T(128)S(6)} %add.435, s32[]{:T(128)S(6)} %add.436, s32[]{:T(128)S(6)} %add.437, ...), kind=kLoop, calls=%fused_computation.8.clone.1 | loop fusion | flops 12320768 | bytes 9699392 | tf_op jit(solution)/shard_map/while/body/eval_jaxpr/add | solution.py:31
  77.6 2.2 reshape.100
  79.8 5.0 fusion.97
  95.3 9.7 multiply_add_fusion.9
  107.2 5.0 fusion.97
  122.7 10.7 %multiply_add_fusion.9 = f32[4,16,4096]{2,1,0:T(8,128)S(1)} fusion(bf16[64,31,4096]{2,1,0:T(8,128)(2,1)} %get-tuple-element.280, s32[]{:T(128)S(6)} %select_n.151, s32[]{:T(128)S(6)} %add.431, s32[]{:T(128)S(6)} %add.432, s32[]{:T(128)S(6)} %add.433, s32[]{:T(128)S(6)} %add.434, s32[]{:T(128)S(6)} %add.435, s32[]{:T(128)S(6)} %add.436, s32[]{:T(128)S(6)} %add.437, ...), kind=kLoop, calls=%fused_computation.8.clone.1 | loop fusion | flops 12320768 | bytes 9699392 | tf_op jit(solution)/shard_map/while/body/eval_jaxpr/add | solution.py:31
  135.6 5.0 fusion.97
  151.2 9.9 %multiply_add_fusion.9 = f32[4,16,4096]{2,1,0:T(8,128)S(1)} fusion(bf16[64,31,4096]{2,1,0:T(8,128)(2,1)} %get-tuple-element.280, s32[]{:T(128)S(6)} %select_n.151, s32[]{:T(128)S(6)} %add.431, s32[]{:T(128)S(6)} %add.432, s32[]{:T(128)S(6)} %add.433, s32[]{:T(128)S(6)} %add.434, s32[]{:T(128)S(6)} %add.435, s32[]{:T(128)S(6)} %add.436, s32[]{:T(128)S(6)} %add.437, ...), kind=kLoop, calls=%fused_computation.8.clone.1 | loop fusion | flops 12320768 | bytes 9699392 | tf_op jit(solution)/shard_map/while/body/eval_jaxpr/add | solution.py:31
  163.3 5.0 fusion.97
  178.8 9.5 multiply_add_fusion.9
  188.3 2.2 reshape.100
  190.6 5.0 fusion.97
  206.1 10.1 %multiply_add_fusion.9 = f32[4,16,4096]{2,1,0:T(8,128)S(1)} fusion(bf16[64,31,4096]{2,1,0:T(8,128)(2,1)} %get-tuple-element.280, s32[]{:T(128)S(6)} %select_n.151, s32[]{:T(128)S(6)} %add.431, s32[]{:T(128)S(6)} %add.432, s32[]{:T(128)S(6)} %add.433, s32[]{:T(128)S(6)} %add.434, s32[]{:T(128)S(6)} %add.435, s32[]{:T(128)S(6)} %add.436, s32[]{:T(128)S(6)} %add.437, ...), kind=kLoop, calls=%fused_computation.8.clone.1 | loop fusion | flops 12320768 | bytes 9699392 | tf_op jit(solution)/shard_map/while/body/eval_jaxpr/add | solution.py:31
  216.2 2.2 reshape.100
  218.4 5.0 fusion.97
  233.9 10.9 %multiply_add_fusion.9 = f32[4,16,4096]{2,1,0:T(8,128)S(1)} fusion(bf16[64,31,4096]{2,1,0:T(8,128)(2,1)} %get-tuple-element.280, s32[]{:T(128)S(6)} %select_n.151, s32[]{:T(128)S(6)} %add.431, s32[]{:T(128)S(6)} %add.432, s32[]{:T(128)S(6)} %add.433, s32[]{:T(128)S(6)} %add.434, s32[]{:T(128)S(6)} %add.435, s32[]{:T(128)S(6)} %add.436, s32[]{:T(128)S(6)} %add.437, ...), kind=kLoop, calls=%fused_computation.8.clone.1 | loop fusion | flops 12320768 | bytes 9699392 | tf_op jit(solution)/shard_map/while/body/eval_jaxpr/add | solution.py:31
  244.8 2.2 reshape.100
  247.0 5.0 fusion.97
  262.6 9.6 multiply_add_fusion.9
  274.3 5.0 fusion.97
  289.9 10.2 %multiply_add_fusion.9 = f32[4,16,4096]{2,1,0:T(8,128)S(1)} fusion(bf16[64,31,4096]{2,1,0:T(8,128)(2,1)} %get-tuple-element.280, s32[]{:T(128)S(6)} %select_n.151, s32[]{:T(128)S(6)} %add.431, s32[]{:T(128)S(6)} %add.432, s32[]{:T(128)S(6)} %add.433, s32[]{:T(128)S(6)} %add.434, s32[]{:T(128)S(6)} %add.435, s32[]{:T(128)S(6)} %add.436, s32[]{:T(128)S(6)} %add.437, ...), kind=kLoop, calls=%fused_computation.8.clone.1 | loop fusion | flops 12320768 | bytes 9699392 | tf_op jit(solution)/shard_map/while/body/eval_jaxpr/add | solution.py:31
  300.0 2.2 reshape.100
  302.3 5.0 fusion.97
  317.8 9.8 multiply_add_fusion.9
  329.8 5.0 fusion.97
  345.3 10.2 %multiply_add_fusion.9 = f32[4,16,4096]{2,1,0:T(8,128)S(1)} fusion(bf16[64,31,4096]{2,1,0:T(8,128)(2,1)} %get-tuple-element.280, s32[]{:T(128)S(6)} %select_n.151, s32[]{:T(128)S(6)} %add.431, s32[]{:T(128)S(6)} %add.432, s32[]{:T(128)S(6)} %add.433, s32[]{:T(128)S(6)} %add.434, s32[]{:T(128)S(6)} %add.435, s32[]{:T(128)S(6)} %add.436, s32[]{:T(128)S(6)} %add.437, ...), kind=kLoop, calls=%fused_computation.8.clone.1 | loop fusion | flops 12320768 | bytes 9699392 | tf_op jit(solution)/shard_map/while/body/eval_jaxpr/add | solution.py:31
  357.8 5.0 fusion.97
  373.3 10.8 %multiply_add_fusion.9 = f32[4,16,4096]{2,1,0:T(8,128)S(1)} fusion(bf16[64,31,4096]{2,1,0:T(8,128)(2,1)} %get-tuple-element.280, s32[]{:T(128)S(6)} %select_n.151, s32[]{:T(128)S(6)} %add.431, s32[]{:T(128)S(6)} %add.432, s32[]{:T(128)S(6)} %add.433, s32[]{:T(128)S(6)} %add.434, s32[]{:T(128)S(6)} %add.435, s32[]{:T(128)S(6)} %add.436, s32[]{:T(128)S(6)} %add.437, ...), kind=kLoop, calls=%fused_computation.8.clone.1 | loop fusion | flops 12320768 | bytes 9699392 | tf_op jit(solution)/shard_map/while/body/eval_jaxpr/add | solution.py:31
  384.1 2.2 reshape.100
  386.3 5.0 fusion.97
  401.8 10.7 %multiply_add_fusion.9 = f32[4,16,4096]{2,1,0:T(8,128)S(1)} fusion(bf16[64,31,4096]{2,1,0:T(8,128)(2,1)} %get-tuple-element.280, s32[]{:T(128)S(6)} %select_n.151, s32[]{:T(128)S(6)} %add.431, s32[]{:T(128)S(6)} %add.432, s32[]{:T(128)S(6)} %add.433, s32[]{:T(128)S(6)} %add.434, s32[]{:T(128)S(6)} %add.435, s32[]{:T(128)S(6)} %add.436, s32[]{:T(128)S(6)} %add.437, ...), kind=kLoop, calls=%fused_computation.8.clone.1 | loop fusion | flops 12320768 | bytes 9699392 | tf_op jit(solution)/shard_map/while/body/eval_jaxpr/add | solution.py:31
  412.6 2.2 reshape.100
  414.8 5.0 fusion.97
  430.3 10.3 %multiply_add_fusion.9 = f32[4,16,4096]{2,1,0:T(8,128)S(1)} fusion(bf16[64,31,4096]{2,1,0:T(8,128)(2,1)} %get-tuple-element.280, s32[]{:T(128)S(6)} %select_n.151, s32[]{:T(128)S(6)} %add.431, s32[]{:T(128)S(6)} %add.432, s32[]{:T(128)S(6)} %add.433, s32[]{:T(128)S(6)} %add.434, s32[]{:T(128)S(6)} %add.435, s32[]{:T(128)S(6)} %add.436, s32[]{:T(128)S(6)} %add.437, ...), kind=kLoop, calls=%fused_computation.8.clone.1 | loop fusion | flops 12320768 | bytes 9699392 | tf_op jit(solution)/shard_map/while/body/eval_jaxpr/add | solution.py:31
  440.6 2.2 reshape.100
  442.8 5.0 fusion.97
  458.3 10.4 %multiply_add_fusion.9 = f32[4,16,4096]{2,1,0:T(8,128)S(1)} fusion(bf16[64,31,4096]{2,1,0:T(8,128)(2,1)} %get-tuple-element.280, s32[]{:T(128)S(6)} %select_n.151, s32[]{:T(128)S(6)} %add.431, s32[]{:T(128)S(6)} %add.432, s32[]{:T(128)S(6)} %add.433, s32[]{:T(128)S(6)} %add.434, s32[]{:T(128)S(6)} %add.435, s32[]{:T(128)S(6)} %add.436, s32[]{:T(128)S(6)} %add.437, ...), kind=kLoop, calls=%fused_computation.8.clone.1 | loop fusion | flops 12320768 | bytes 9699392 | tf_op jit(solution)/shard_map/while/body/eval_jaxpr/add | solution.py:31
  468.7 2.2 reshape.100
  470.9 5.0 fusion.97
  486.4 10.1 %multiply_add_fusion.9 = f32[4,16,4096]{2,1,0:T(8,128)S(1)} fusion(bf16[64,31,4096]{2,1,0:T(8,128)(2,1)} %get-tuple-element.280, s32[]{:T(128)S(6)} %select_n.151, s32[]{:T(128)S(6)} %add.431, s32[]{:T(128)S(6)} %add.432, s32[]{:T(128)S(6)} %add.433, s32[]{:T(128)S(6)} %add.434, s32[]{:T(128)S(6)} %add.435, s32[]{:T(128)S(6)} %add.436, s32[]{:T(128)S(6)} %add.437, ...), kind=kLoop, calls=%fused_computation.8.clone.1 | loop fusion | flops 12320768 | bytes 9699392 | tf_op jit(solution)/shard_map/while/body/eval_jaxpr/add | solution.py:31
  498.7 5.0 fusion.97
  513.9 28.6 %copy.46 = bf16[2,2048,64,16]{2,3,0,1:T(8,128)(2,1)} copy(bf16[2,2048,64,16]{1,3,2,0:T(8,128)(2,1)} %get-tuple-element.135) | data formatting | bytes 16777216 | tf_op jit(solution)/shard_map/while | solution.py:93
  542.5 14.5 %bitcast_bitcast_fusion = bf16[2048,1,2,16,64]{4,3,2,1,0:T(8,128)(2,1)} fusion(bf16[2,2048,64,16]{2,3,0,1:T(8,128)(2,1)} %copy.46), kind=kLoop, calls=%fused_computation.87 | loop fusion | bytes 16777216
  557.0 19.6 %reshape.97 = bf16[16,2,131072]{2,1,0:T(2,128)(2,1)} reshape(bf16[2048,1,2,16,64]{4,3,2,1,0:T(8,128)(2,1)} %bitcast_bitcast_fusion) | data formatting | bytes 16777216
  576.6 81.2 %all-to-all-start = ((bf16[16,2,131072]{2,1,0:T(2,128)(2,1)}), bf16[16,2,131072]{2,1,0:T(2,128)(2,1)}, u32[]{:S(2)}, u32[]{:S(2)}) async-start(bf16[16,2,131072]{2,1,0:T(2,128)(2,1)} %reshape.97), calls=%async_computation | async-start | bytes 16777216 | tf_op jit(solution)/shard_map/all_to_all | solution.py:98
  657.9 182.3 %all-to-all-done = bf16[16,2,131072]{2,1,0:T(2,128)(2,1)} async-done(((bf16[16,2,131072]{2,1,0:T(2,128)(2,1)}), bf16[16,2,131072]{2,1,0:T(2,128)(2,1)}, u32[]{:S(2)}, u32[]{:S(2)}) %all-to-all-start) | async-done | bytes 8388640 | tf_op jit(solution)/shard_map/all_to_all | solution.py:98
  840.2 19.2 %reshape.98 = bf16[2048,1,2,16,64]{4,3,2,1,0:T(8,128)(2,1)} reshape(bf16[16,2,131072]{2,1,0:T(2,128)(2,1)} %all-to-all-done) | data formatting | bytes 16777216
  859.4 20.7 %copy.60 = bf16[1,2,16,128,64,16]{3,2,5,4,1,0:T(8,128)(2,1)} copy(bf16[1,2,16,128,64,16]{4,5,1,3,2,0:T(8,128)(2,1)} %bitcast.98) | data formatting | bytes 16777216 | tf_op jit(solution)/shard_map/all_to_all | solution.py:98
  880.1 8.9 copy.48
  889.0 5.5 fusion.70
  894.5 3.2 copy.50
  897.8 7.3 copy.52
  905.1 5.4 copy.49
  910.5 7.4 copy.51
  917.9 5.5 neg.14
  923.4 32.7 %fusion.57 = f32[128,512,256]{2,1,0:T(8,128)} fusion(bf16[128,256,64]{1,2,0:T(8,128)(2,1)} %neg.14, bf16[128,256,64]{1,2,0:T(8,128)(2,1)} %copy.52, bf16[128,256,64]{1,2,0:T(8,128)(2,1)} %copy.51), kind=kOutput, calls=%fused_computation.72 | convolution fusion | flops 4378853376 | bytes 79691776 | tf_op jit(solution)/shard_map/cif,cjf->cij/dot_general | solution.py:19
  956.1 33.5 %fusion.56 = f32[128,256,256]{2,1,0:T(8,128)} fusion(f32[128,512,256]{2,1,0:T(8,128)} %fusion.57, pred[256,256]{1,0:T(8,128)(4,1)S(1)} %iota_compare_fusion), kind=kLoop, calls=%fused_computation.70 | loop fusion | flops 16777216 | bytes 100728832 | tf_op jit(solution)/shard_map/mul | solution.py:24
  (171 shorter events, 183.6 us)
Async XLA Ops:
  21.5 14.8 %collective-permute-start = (bf16[64,15,4096]{2,0,1:T(8,128)(2,1)}, bf16[64,15,4096]{2,0,1:T(8,128)(2,1)}, u32[]{:S(2)}, u32[]{:S(2)}) collective-permute-start(bf16[64,15,4096]{2,0,1:T(8,128)(2,1)} %copy.61), channel_id=1, source_target_pairs={{0,1},{1,2},{2,3},{4,5},{5,6},{6,7},{8,9},{9,10},{10,11},{12,13},{... | collective-permute-start | bytes 23592968 | tf_op jit(solution)/shard_map/ppermute | solution.py:12
  62.1 4.3 copy-start
  576.6 263.5 %all-to-all-start = ((bf16[16,2,131072]{2,1,0:T(2,128)(2,1)}), bf16[16,2,131072]{2,1,0:T(2,128)(2,1)}, u32[]{:S(2)}, u32[]{:S(2)}) async-start(bf16[16,2,131072]{2,1,0:T(2,128)(2,1)} %reshape.97), calls=%async_computation | async-start | bytes 16777216 | tf_op jit(solution)/shard_map/all_to_all | solution.py:98
where the time goes:
time: 999 us; the launch traced here: 990 us
  other arithmetic  252 us (25%)
  local copies, waits for them, and re-layouts  241 us (24%)
  matrix products  216 us (22%)
  waiting for transfers between devices  196 us (20%)
  starting transfers between devices  82.7 us (8%)
    all_to_all x1, waiting for transfers between devices, per_device(): lax.all_to_all(local_spec[None], ('inp', 'tm', 'pol'), split_axis=2, conc...  182 us
    add x16, other arithmetic, filter_frames(): total + coefficients[tap_index] * block[:, tap_index:tap_index + frame_co...  163 us
    all_to_all x1, starting transfers between devices, per_device(): lax.all_to_all(local_spec[None], ('inp', 'tm', 'pol'), split_axis=2, conc...  81.2 us
    dot_general x16, matrix products, transform(): jnp.einsum('rab,ak->rbk', blocks, table_one, precision=lax.Precision.HIGH...  80.8 us
    unnamed x6, local copies, waits for them, and re-layouts  64.4 us
    reshape x16, local copies, waits for them, and re-layouts, transform(): blocks = filtered.reshape(row_total, inner_len, outer_len)  35.3 us
    mul x1, other arithmetic, correlate(): return packed * (1.0 / total_frames)  33.5 us
    dot_general x1, matrix products, correlate(): jnp.einsum('cif,cjf->cij', stacked, joined, preferred_element_type=jnp.fl...  32.7 us
  transfers between devices with their start and end apart: 2, of which 2 were waited for; matrix products, arithmetic and copies ran while one was open for 0% of the time, Pallas kernels for 0%

commit v1 on v0

--- a/solution.py
+++ b/solution.py
@@ -1,9 +1,20 @@
+import functools
 import math
 
 import jax
 import jax.numpy as jnp
+import ml_dtypes
+import numpy as np
 from jax import lax
+from jax.experimental import pallas as pl
+from jax.experimental.pallas import tpu as pltpu
 from jax.sharding import PartitionSpec as P
+
+RADIX = 16
+GROUPS = RADIX // 2
+LANES = 128
+ROWS = 8
+MIB = 1 << 20
 
 
 def from_behind(block, axis, distance):
@@ -71,7 +82,7 @@
     return jnp.stack([out_re, out_im]).reshape(2, length // 2, row_total) * scale_factor
 
 
-def per_device(samples, coefficients):
+def general(samples, coefficients):
     in_dev, frame_count, length = samples.shape
     taps = coefficients.shape[0]
     channels = length // 2
@@ -106,6 +117,310 @@
     return correlate(arrived[0], arrived[1], total_frames)
 
 
+@functools.lru_cache(maxsize=None)
+def fourier_tables(length, owners):
+    span = length // RADIX
+    per_owner = length // 2 // owners // RADIX
+    run = 2 * per_owner
+    slots = LANES // run
+    place = np.arange(span, dtype=np.int64)
+    tables = np.zeros((GROUPS, 2 * span, 2 * owners * run))
+    for group in range(GROUPS):
+        for owner in range(owners):
+            block, inside = divmod(owner, slots)
+            column = block * LANES + ((inside - group) % slots) * run
+            for side in range(2):
+                residue = side * GROUPS if group == 0 else (group, RADIX - group)[side]
+                channel = RADIX * (owner * per_owner + np.arange(per_owner)) + residue
+                angle = 2.0 * np.pi * (place[:, None] * channel[None, :] % length) / length
+                cos, sin = np.cos(angle) / math.sqrt(length), np.sin(angle) / math.sqrt(length)
+                re = slice(column + side * per_owner, column + (side + 1) * per_owner)
+                im = slice(re.start + owners * run, re.stop + owners * run)
+                if group == 0:
+                    rows = slice(side * span, (side + 1) * span)
+                    tables[group, rows, re] = cos
+                    tables[group, rows, im] = -sin
+                else:
+                    sign = 1.0 - 2.0 * side
+                    tables[group, :span, re] = cos
+                    tables[group, span:, re] = sign * sin
+                    tables[group, :span, im] = -sin
+                    tables[group, span:, im] = sign * cos
+    exact = tables.astype(np.float32)
+    high = exact.astype(ml_dtypes.bfloat16)
+    low = (exact - high.astype(np.float32)).astype(ml_dtypes.bfloat16)
+    return np.stack([high, low], axis=1)
+
+
+def real_fourier(values):
+    count = len(values)
+    if count == 1:
+        return [(values[0], None)]
+    if count == 2:
+        return [(values[0] + values[1], None), (values[0] - values[1], None)]
+    even, odd = real_fourier(values[0::2]), real_fourier(values[1::2])
+    bins = [None] * (count // 2 + 1)
+    bins[0] = (even[0][0] + odd[0][0], None)
+    bins[count // 2] = (even[0][0] - odd[0][0], None)
+    bins[count // 4] = (even[count // 4][0], -odd[count // 4][0])
+    for k in range(1, count // 4):
+        (er, ei), (pr, pi) = even[k], odd[k]
+        if 8 * k == count:
+            half = math.sqrt(0.5)
+            tr, ti = (pr + pi) * half, (pi - pr) * half
+        else:
+            c, s = math.cos(2 * math.pi * k / count), math.sin(2 * math.pi * k / count)
+            tr, ti = pr * c + pi * s, pi * c - pr * s
+        bins[k] = (er + tr, ei + ti)
+        bins[count // 2 - k] = (er - tr, ti - ei)
+    return bins
+
+
+def filter_bank_kernel(
+    steps, own_ref, old_ref, coef_ref, table_hbm, out_ref, frames_ref, kept_ref, high_ref, low_ref, spec_ref, table_ref, sem
+):
+    inputs, frames, length = own_ref.shape
+    taps = coef_ref.shape[0]
+    span = length // RADIX
+    parts = span // LANES
+    step = pl.program_id(0)
+    copy = pltpu.make_async_copy(table_hbm, table_ref, sem)
+
+    @pl.when(step == 0)
+    def _():
+        copy.start()
+
+    base = step * inputs * frames
+
+    def one_block(block, carry):
+        lanes = pl.ds(pl.multiple_of(block * LANES, LANES), LANES)
+        for i in range(inputs):
+            frames_ref[pl.ds(2 * frames * i, frames), :] = old_ref[i, :, lanes].astype(jnp.float32)
+            frames_ref[pl.ds(2 * frames * i + frames, frames), :] = own_ref[i, :, lanes].astype(jnp.float32)
+        taps_now = [jnp.broadcast_to(coef_ref[t : t + 1, lanes], (ROWS, LANES)) for t in range(taps)]
+        first = frames - taps + 1
+        totals = [None] * frames
+        for row in range(first, 2 * frames):
+            value = frames_ref[pl.ds(row, inputs, stride=2 * frames), :]
+            for f in range(max(0, row - first - taps + 1), min(frames, row - first + 1)):
+                term = taps_now[row - first - f] * value
+                totals[f] = term if totals[f] is None else totals[f] + term
+        for f in range(frames):
+            kept_ref[block, pl.ds(f, inputs, stride=frames), :] = totals[f]
+        return carry
+
+    lax.fori_loop(0, length // LANES, one_block, 0)
+
+    def one_rows(index, carry):
+        part = index % parts
+        first = pl.multiple_of(index // parts * 16, 16)
+        values = [kept_ref[parts * j + part, pl.ds(first, 16), :] for j in range(RADIX)]
+        bins = real_fourier(values)
+        rows = pl.ds(pl.multiple_of(base + first, 16), 16)
+        for group in range(GROUPS):
+            pair = (bins[0][0], bins[GROUPS][0]) if group == 0 else bins[group]
+            for half in range(2):
+                lanes = pl.ds(pl.multiple_of(half * span + part * LANES, LANES), LANES)
+                top = pair[half].astype(jnp.bfloat16)
+                high_ref[group, rows, lanes] = top
+                low_ref[group, rows, lanes] = (pair[half] - top.astype(jnp.float32)).astype(jnp.bfloat16)
+        return carry
+
+    lax.fori_loop(0, parts * inputs * frames // 16, one_rows, 0)
+
+    @pl.when(step == steps - 1)
+    def _():
+        copy.wait()
+
+        def one_group(group, carry):
+            top, rest = high_ref[group], low_ref[group]
+            total = jnp.dot(top, table_ref[group, 0], preferred_element_type=jnp.float32)
+            total = total + jnp.dot(rest, table_ref[group, 0], preferred_element_type=jnp.float32)
+            total = total + jnp.dot(top, table_ref[group, 1], preferred_element_type=jnp.float32)
+            spec_ref[group] = total
+            return carry
+
+        lax.fori_loop(0, GROUPS, one_group, 0)
+        owners = out_ref.shape[0]
+        slots = GROUPS
+        run = LANES // slots
+
+        def one_part(index, carry):
+            first = pl.multiple_of(index * 16, 16)
+            slot = lax.broadcasted_iota(jnp.int32, (16, LANES), 1) // run
+            picks = [(slot // (1 << bit)) % 2 == 1 for bit in range(3)]
+            for kind in range(2):
+                for block in range(owners // slots):
+                    lanes = pl.ds((kind * (owners // slots) + block) * LANES, LANES)
+                    now = [spec_ref[group, pl.ds(first, 16), lanes] for group in range(GROUPS)]
+                    for bit in range(3):
+                        now = [jnp.where(picks[bit], now[(e - (1 << bit)) % slots], now[e]) for e in range(slots)]
+                    for inside in range(slots):
+                        out_ref[block * slots + inside, pl.ds(first, 16), pl.ds(kind * LANES, LANES)] = now[inside].astype(jnp.bfloat16)
+            return carry
+
+        lax.fori_loop(0, out_ref.shape[1] // 16, one_part, 0)
+
+
+def filter_bank(samples, history, coefficients, table, first, count, owners):
+    _, frames, length = samples.shape
+    steps = count // ROWS
+    rows = count * frames
+    offset = first // ROWS
+    return pl.pallas_call(
+        functools.partial(filter_bank_kernel, steps),
+        out_shape=jax.ShapeDtypeStruct((owners, rows, 2 * LANES), jnp.bfloat16),
+        grid=(steps,),
+        in_specs=[
+            pl.BlockSpec((ROWS, frames, length), lambda i: (i + offset, 0, 0)),
+            pl.BlockSpec((ROWS, frames, length), lambda i: (i, 0, 0)),
+            pl.BlockSpec(coefficients.shape, lambda i: (0, 0), pipeline_mode=pl.Buffered(1)),
+            pl.BlockSpec(memory_space=pl.ANY),
+        ],
+        out_specs=pl.BlockSpec((owners, rows, 2 * LANES), lambda i: (0, 0, 0), pipeline_mode=pl.Buffered(1)),
+        scratch_shapes=[
+            pltpu.VMEM((2 * ROWS * frames, LANES), jnp.float32),
+            pltpu.VMEM((length // LANES, ROWS * frames, LANES), jnp.float32),
+            pltpu.VMEM((GROUPS, rows, 2 * length // RADIX), jnp.bfloat16),
+            pltpu.VMEM((GROUPS, rows, 2 * length // RADIX), jnp.bfloat16),
+            pltpu.VMEM((GROUPS, rows, 2 * owners * LANES // GROUPS), jnp.float32),
+            pltpu.VMEM(table.shape, jnp.bfloat16),
+            pltpu.SemaphoreType.DMA,
+        ],
+        compiler_params=pltpu.CompilerParams(vmem_limit_bytes=56 * MIB),
+        cost_estimate=pl.CostEstimate(flops=rows * length * 512 * 3, bytes_accessed=16 * MIB, transcendentals=0),
+        name="filter_bank",
+    )(samples, history, coefficients, table)
+
+
+def turn_kernel(frames, in_ref, out_ref, work_ref):
+    blocks, rows, _ = in_ref.shape
+    count = rows // frames
+
+    def one_input(i, carry):
+        first = pl.multiple_of(i * frames, frames)
+        pieces = [
+            in_ref[t, pl.ds(first, frames), pl.ds(kind * LANES, LANES)]
+            for kind in range(2)
+            for t in range(blocks)
+        ]
+        square = jnp.concatenate(pieces, axis=0).astype(jnp.float32)
+        work_ref[pl.ds(i, LANES, stride=count), :] = square.T
+        return carry
+
+    lax.fori_loop(0, count, one_input, 0)
+    out_ref[...] = work_ref[...].reshape(LANES, count, LANES).astype(jnp.bfloat16)
+
+
+def turn(arrived, sets, frames):
+    sources, rows, _ = arrived.shape
+    blocks = sources // sets
+    count = rows // frames
+    return pl.pallas_call(
+        functools.partial(turn_kernel, frames),
+        out_shape=jax.ShapeDtypeStruct((LANES, sets * count, LANES), jnp.bfloat16),
+        grid=(sets,),
+        in_specs=[pl.BlockSpec((blocks, rows, 2 * LANES), lambda z: (z, 0, 0))],
+        out_specs=pl.BlockSpec((LANES, count, LANES), lambda z: (0, z, 0)),
+        scratch_shapes=[pltpu.VMEM((LANES * count, LANES), jnp.float32)],
+        compiler_params=pltpu.CompilerParams(vmem_limit_bytes=56 * MIB),
+        cost_estimate=pl.CostEstimate(flops=4 * arrived.size, bytes_accessed=4 * arrived.size, transcendentals=0),
+        name="turn",
+    )(arrived)
+
+
+def correlate_kernel(counts, sets, scale, order_ref, *refs):
+    *in_refs, out_ref = refs
+    held = out_ref.shape[0]
+
+    def one_channel(u, carry):
+        joined = jnp.concatenate(
+            [
+                in_ref[u, pl.ds(z * count, count), :]
+                for z in range(sets)
+                for in_ref, count in zip(in_refs, counts)
+            ],
+            axis=0,
+        )
+        lane = lax.broadcasted_iota(jnp.int32, joined.shape, 1)
+        wide = pltpu.roll(joined.astype(jnp.float32), LANES // 2, 1)
+        turned = jnp.where(lane < LANES // 2, wide, -wide).astype(jnp.bfloat16)
+        across = (((1,), (1,)), ((), ()))
+        real = lax.dot_general(joined, joined, across, preferred_element_type=jnp.float32)
+        imag = lax.dot_general(turned, joined, across, preferred_element_type=jnp.float32)
+        row = lax.broadcasted_iota(jnp.int32, real.shape, 0)
+        col = lax.broadcasted_iota(jnp.int32, real.shape, 1)
+        out_ref[u, 0] = jnp.where(row <= col, real, imag) * scale
+        return carry
+
+    lax.fori_loop(0, held, one_channel, 0)
+
+
+def correlate_all(turned, counts, sets, order, scale):
+    channels = turned[0].shape[0]
+    held = channels // RADIX
+    width = sets * sum(counts)
+    out = pl.pallas_call(
+        functools.partial(correlate_kernel, counts, sets, scale),
+        out_shape=jax.ShapeDtypeStruct((held, RADIX, width, width), jnp.float32),
+        grid_spec=pltpu.PrefetchScalarGridSpec(
+            num_scalar_prefetch=1,
+            grid=(RADIX,),
+            in_specs=[pl.BlockSpec((held, sets * count, LANES), lambda s, order: (s, 0, 0)) for count in counts],
+            out_specs=pl.BlockSpec((held, 1, width, width), lambda s, order: (0, order[s], 0, 0)),
+        ),
+        compiler_params=pltpu.CompilerParams(vmem_limit_bytes=56 * MIB),
+        cost_estimate=pl.CostEstimate(
+            flops=4 * channels * width * width * LANES, bytes_accessed=40 * MIB, transcendentals=0
+        ),
+        name="correlate",
+    )(order, *turned)
+    return out.reshape(channels, width, width)
+
+
+def plan(in_dev):
+    return [in_dev // 4] * 4
+
+
+def fast(samples, coefficients):
+    in_dev, frames, length = samples.shape
+    everyone = ("inp", "tm", "pol")
+    owners = lax.axis_size(everyone)
+    sets = lax.axis_size("inp")
+    total_frames = frames * owners // sets
+    table = jnp.asarray(fourier_tables(length, owners))
+    counts = plan(in_dev)
+    starts = [sum(counts[:k]) for k in range(len(counts))]
+    slot = lax.axis_index(everyone) % GROUPS
+    steps = jnp.arange(RADIX, dtype=jnp.int32)
+    group, side = (slot - steps // 2) % GROUPS, steps % 2
+    order = jnp.where(group == 0, side * GROUPS, jnp.where(side == 0, group, RADIX - group)).astype(jnp.int32)
+    turned = []
+    for first, count in zip(starts, counts):
+        history = from_behind(samples[first : first + count], ("tm", "pol"), 1)
+        spectra = filter_bank(samples, history, coefficients, table, first, count, owners)
+        arrived = lax.all_to_all(spectra, everyone, 0, 0, tiled=True)
+        turned.append(turn(arrived, sets, frames))
+    return correlate_all(turned, counts, sets, order, 1.0 / total_frames)
+
+
+def per_device(samples, coefficients):
+    in_dev, frames, length = samples.shape
+    taps = coefficients.shape[0]
+    owners = lax.axis_size(("inp", "tm", "pol"))
+    blocks = lax.axis_size(("tm", "pol"))
+    fits = (
+        frames == 16
+        and taps <= frames + 1
+        and in_dev % (4 * ROWS) == 0
+        and length == 2 * LANES * owners
+        and length % (RADIX * LANES) == 0
+        and owners % GROUPS == 0
+        and 2 * blocks * frames == LANES
+    )
+    return fast(samples, coefficients) if fits else general(samples, coefficients)
+
+
 def solution(mesh):
     placed = (P(("grp", "inp"), ("tm", "pol"), None), P())
     return jax.shard_map(

time: 999 us -> 372 us (0.37)
  other arithmetic: 252 us -> 0.58 us
  local copies, waits for them, and re-layouts: 241 us -> 13.7 us
  matrix products: 216 us -> 0 us
  Pallas kernels: 0 us -> 147 us
  waiting for transfers between devices: 196 us -> 104 us
  starting transfers between devices: 82.7 us -> 106 us
    dot_general x81 -> x0, matrix products: 216 us -> none  [the longest x16 80.8 us: transform(): jnp.einsum('rab,ak->rbk', blocks, table_one, precision=lax.Precision.HIGH...]
    add x16 -> x0, other arithmetic: 163 us -> none  [filter_frames(): total + coefficients[tap_index] * block[:, tap_index:tap_index + frame_co...]
    pallas_call x0 -> x9, Pallas kernels: none -> 147 us  [the longest x4 75.3 us: filter_bank(): pl.pallas_call(functools.partial(filter_bank_kernel, steps), out_shape=ja...]
    all_to_all x1 -> x4, waiting for transfers between devices: 182 us -> 83.9 us  [fast(): arrived = lax.all_to_all(spectra, everyone, 0, 0, tiled=True)]
    unnamed x6 -> x12, local copies, waits for them, and re-layouts: 64.4 us -> 8 us
    reshape x16 -> x0, local copies, waits for them, and re-layouts: 35.3 us -> none  [transform(): blocks = filtered.reshape(row_total, inner_len, outer_len)]
    mul x1 -> x0, other arithmetic: 33.5 us -> none  [correlate(): return packed * (1.0 / total_frames)]
    dynamic_update_slice x16 -> x0, other arithmetic: 30.5 us -> none  [one_group(): lax.dynamic_update_slice_in_dim(buffer_now, spectra_grp, group_index * gr...]
  transfers between devices with their start and end apart: 2 -> 8, of which waited for: 2 -> 8; matrix products, arithmetic and copies ran while one was open for 0% -> 0% of each run, Pallas kernels for 0% -> 22%
where the time goes in v1:
time: 372 us
  Pallas kernels  147 us (40%)
  starting transfers between devices  106 us (28%)
  waiting for transfers between devices  104 us (28%)
  local copies, waits for them, and re-layouts  13.7 us (4%)
    all_to_all x4, starting transfers between devices, fast(): arrived = lax.all_to_all(spectra, everyone, 0, 0, tiled=True)  101 us
    all_to_all x4, waiting for transfers between devices, fast(): arrived = lax.all_to_all(spectra, everyone, 0, 0, tiled=True)  83.9 us
    pallas_call x4, Pallas kernels, filter_bank(): pl.pallas_call(functools.partial(filter_bank_kernel, steps), out_shape=ja...  75.3 us
    pallas_call x1, Pallas kernels, correlate_all(): pl.pallas_call(functools.partial(correlate_kernel, counts, sets, scale),...  37.1 us
    pallas_call x4, Pallas kernels, turn(): pl.pallas_call(functools.partial(turn_kernel, frames), out_shape=jax.Shap...  34.8 us
    ppermute x4, waiting for transfers between devices, from_behind(): return lax.ppermute(block, axis, route)  19.8 us
    unnamed x12, local copies, waits for them, and re-layouts  8 us
  transfers between devices with their start and end apart: 8, of which 8 were waited for; matrix products, arithmetic and copies ran while one was open for 0% of the time, Pallas kernels for 22%

profile of v1, /device:TPU:15, one launch (start us, length us, event | category | flops | bytes accessed | tf_op | source)
XLA Modules:
  0.0 371.8 jit_solution(2231851898739536697)
XLA Ops:
  0.0 5.7 %fusion.2 = (bf16[16,16,4096]{2,1,0:T(8,128)(2,1)S(1)}, bf16[16,16,4096]{2,1,0:T(8,128)(2,1)}, bf16[16,16,4096]{2,1,0:T(8,128)(2,1)}, bf16[16,16,4096]{2,1,0:T(8,128)(2,1)}) fusion(bf16[64,16,4096]{2,1,0:T(8,128)(2,1)} %own_ref.7), kind=kLoop, calls=%fused_computation.12 | loop fusion | bytes 16777216 | tf_op jit(solution)/shard_map/slice | solution.py:400
  5.7 1.3 collective-permute-start.3
  7.0 4.9 %collective-permute-done.3.old_ref = bf16[16,16,4096]{2,1,0:T(8,128)(2,1)S(1)} collective-permute-done((bf16[16,16,4096]{2,1,0:T(8,128)(2,1)S(1)}, bf16[16,16,4096]{2,1,0:T(8,128)(2,1)S(1)}, u32[]{:S(2)}, u32[]{:S(2)}) %collective-permute-start.3) | collective-permute-done | bytes 2097184 | tf_op jit(solution)/shard_map/ppermute | solution.py:23
  11.9 0.0 copy-start.3
  11.9 1.4 copy-done.3
  13.3 18.8 %filter_bank.7 = bf16[16,256,256]{2,1,0:T(8,128)(2,1)} custom-call(bf16[64,16,4096]{2,1,0:T(8,128)(2,1)} %own_ref.7, bf16[16,16,4096]{2,1,0:T(8,128)(2,1)} %copy-done.3, f32[16,4096]{1,0:T(8,128)} %coef_ref.7, bf16[8,2,512,512]{3,2,1,0:T(8,128)(2,1)} %constant.65.clone.table_hbm), custom_call_target="tpu_custom_call" | custom-call | flops 1610612736 | bytes 16777216 | tf_op jit(solution)/shard_map/filter_bank/pallas_call | solution.py:270
  32.1 27.7 %all-to-all-start.3 = ((bf16[16,256,256]{2,1,0:T(8,128)(2,1)}), bf16[16,256,256]{2,1,0:T(8,128)(2,1)S(1)}, u32[]{:S(2)}, u32[]{:S(2)}) async-start(bf16[16,256,256]{2,1,0:T(8,128)(2,1)} %filter_bank.7), calls=%async_computation.3 | async-start | bytes 4194304 | tf_op jit(solution)/shard_map/all_to_all | solution.py:402
  59.8 1.3 collective-permute-start.2
  61.1 5.0 %collective-permute-done.2.old_ref = bf16[16,16,4096]{2,1,0:T(8,128)(2,1)S(1)} collective-permute-done((bf16[16,16,4096]{2,1,0:T(8,128)(2,1)}, bf16[16,16,4096]{2,1,0:T(8,128)(2,1)S(1)}, u32[]{:S(2)}, u32[]{:S(2)}) %collective-permute-start.2) | collective-permute-done | bytes 2097184 | tf_op jit(solution)/shard_map/ppermute | solution.py:23
  66.0 0.0 copy-start.4
  66.0 1.3 copy-done.4
  67.4 18.9 %filter_bank.6 = bf16[16,256,256]{2,1,0:T(8,128)(2,1)} custom-call(bf16[64,16,4096]{2,1,0:T(8,128)(2,1)} %own_ref.7, bf16[16,16,4096]{2,1,0:T(8,128)(2,1)} %copy-done.4, f32[16,4096]{1,0:T(8,128)} %coef_ref.7, bf16[8,2,512,512]{3,2,1,0:T(8,128)(2,1)} %constant.65.clone.table_hbm), custom_call_target="tpu_custom_call" | custom-call | flops 1610612736 | bytes 16777216 | tf_op jit(solution)/shard_map/filter_bank/pallas_call | solution.py:270
  86.2 21.0 %all-to-all-done.3.in_ref = bf16[16,256,256]{2,1,0:T(8,128)(2,1)S(1)} async-done(((bf16[16,256,256]{2,1,0:T(8,128)(2,1)}), bf16[16,256,256]{2,1,0:T(8,128)(2,1)S(1)}, u32[]{:S(2)}, u32[]{:S(2)}) %all-to-all-start.3) | async-done | bytes 2097184 | tf_op jit(solution)/shard_map/all_to_all | solution.py:402
  107.2 0.0 copy-start
  107.2 1.4 copy-done
  108.6 24.6 %all-to-all-start.2 = ((bf16[16,256,256]{2,1,0:T(8,128)(2,1)}), bf16[16,256,256]{2,1,0:T(8,128)(2,1)}, u32[]{:S(2)}, u32[]{:S(2)}) async-start(bf16[16,256,256]{2,1,0:T(8,128)(2,1)} %filter_bank.6), calls=%async_computation.2 | async-start | bytes 4194304 | tf_op jit(solution)/shard_map/all_to_all | solution.py:402
  133.2 1.3 collective-permute-start.1
  134.5 5.0 %collective-permute-done.1.old_ref = bf16[16,16,4096]{2,1,0:T(8,128)(2,1)S(1)} collective-permute-done((bf16[16,16,4096]{2,1,0:T(8,128)(2,1)}, bf16[16,16,4096]{2,1,0:T(8,128)(2,1)S(1)}, u32[]{:S(2)}, u32[]{:S(2)}) %collective-permute-start.1) | collective-permute-done | bytes 2097184 | tf_op jit(solution)/shard_map/ppermute | solution.py:23
  139.4 0.0 copy-start.5
  139.4 1.3 copy-done.5
  140.7 18.8 %filter_bank.5 = bf16[16,256,256]{2,1,0:T(8,128)(2,1)} custom-call(bf16[64,16,4096]{2,1,0:T(8,128)(2,1)} %own_ref.7, bf16[16,16,4096]{2,1,0:T(8,128)(2,1)} %copy-done.5, f32[16,4096]{1,0:T(8,128)} %coef_ref.7, bf16[8,2,512,512]{3,2,1,0:T(8,128)(2,1)} %constant.65.clone.table_hbm), custom_call_target="tpu_custom_call" | custom-call | flops 1610612736 | bytes 16777216 | tf_op jit(solution)/shard_map/filter_bank/pallas_call | solution.py:270
  159.6 21.1 %all-to-all-done.2.in_ref = bf16[16,256,256]{2,1,0:T(8,128)(2,1)} async-done(((bf16[16,256,256]{2,1,0:T(8,128)(2,1)}), bf16[16,256,256]{2,1,0:T(8,128)(2,1)}, u32[]{:S(2)}, u32[]{:S(2)}) %all-to-all-start.2) | async-done | bytes 2097184 | tf_op jit(solution)/shard_map/all_to_all | solution.py:402
  180.7 24.5 %all-to-all-start.1 = ((bf16[16,256,256]{2,1,0:T(8,128)(2,1)}), bf16[16,256,256]{2,1,0:T(8,128)(2,1)S(1)}, u32[]{:S(2)}, u32[]{:S(2)}) async-start(bf16[16,256,256]{2,1,0:T(8,128)(2,1)} %filter_bank.5), calls=%async_computation.1 | async-start | bytes 4194304 | tf_op jit(solution)/shard_map/all_to_all | solution.py:402
  205.2 1.3 collective-permute-start
  206.4 5.0 %collective-permute-done.old_ref = bf16[16,16,4096]{2,1,0:T(8,128)(2,1)S(1)} collective-permute-done((bf16[16,16,4096]{2,1,0:T(8,128)(2,1)}, bf16[16,16,4096]{2,1,0:T(8,128)(2,1)S(1)}, u32[]{:S(2)}, u32[]{:S(2)}) %collective-permute-start) | collective-permute-done | bytes 2097184 | tf_op jit(solution)/shard_map/ppermute | solution.py:23
  211.4 0.0 copy-start.2
  211.4 1.3 copy-done.2
  212.7 18.8 %filter_bank.4 = bf16[16,256,256]{2,1,0:T(8,128)(2,1)} custom-call(bf16[64,16,4096]{2,1,0:T(8,128)(2,1)} %own_ref.7, bf16[16,16,4096]{2,1,0:T(8,128)(2,1)} %copy-done.2, f32[16,4096]{1,0:T(8,128)} %coef_ref.7, bf16[8,2,512,512]{3,2,1,0:T(8,128)(2,1)} %constant.65.clone.table_hbm), custom_call_target="tpu_custom_call" | custom-call | flops 1610612736 | bytes 16777216 | tf_op jit(solution)/shard_map/filter_bank/pallas_call | solution.py:270
  231.6 21.0 %all-to-all-done.1.in_ref = bf16[16,256,256]{2,1,0:T(8,128)(2,1)S(1)} async-done(((bf16[16,256,256]{2,1,0:T(8,128)(2,1)}), bf16[16,256,256]{2,1,0:T(8,128)(2,1)S(1)}, u32[]{:S(2)}, u32[]{:S(2)}) %all-to-all-start.1) | async-done | bytes 2097184 | tf_op jit(solution)/shard_map/all_to_all | solution.py:402
  252.6 0.0 copy-start.1
  252.6 1.3 copy-done.1
  253.9 24.6 %all-to-all-start = ((bf16[16,256,256]{2,1,0:T(8,128)(2,1)}), bf16[16,256,256]{2,1,0:T(8,128)(2,1)}, u32[]{:S(2)}, u32[]{:S(2)}) async-start(bf16[16,256,256]{2,1,0:T(8,128)(2,1)} %filter_bank.4), calls=%async_computation | async-start | bytes 4194304 | tf_op jit(solution)/shard_map/all_to_all | solution.py:402
  278.5 0.6 compare_select_fusion.3.order_ref
  279.1 8.7 %turn.7.refs_3_ = bf16[128,64,128]{2,1,0:T(8,128)(2,1)} custom-call(bf16[16,256,256]{2,1,0:T(8,128)(2,1)} %copy-done), custom_call_target="tpu_custom_call" | custom-call | flops 4194304 | bytes 4194304 | tf_op jit(solution)/shard_map/turn/pallas_call | solution.py:319
  287.8 8.7 %turn.6.refs_2_ = bf16[128,64,128]{2,1,0:T(8,128)(2,1)} custom-call(bf16[16,256,256]{2,1,0:T(8,128)(2,1)} %all-to-all-done.2.in_ref), custom_call_target="tpu_custom_call" | custom-call | flops 4194304 | bytes 4194304 | tf_op jit(solution)/shard_map/turn/pallas_call | solution.py:319
  296.5 8.7 %turn.5.refs_1_ = bf16[128,64,128]{2,1,0:T(8,128)(2,1)} custom-call(bf16[16,256,256]{2,1,0:T(8,128)(2,1)} %copy-done.1), custom_call_target="tpu_custom_call" | custom-call | flops 4194304 | bytes 4194304 | tf_op jit(solution)/shard_map/turn/pallas_call | solution.py:319
  305.2 20.8 %all-to-all-done.in_ref = bf16[16,256,256]{2,1,0:T(8,128)(2,1)} async-done(((bf16[16,256,256]{2,1,0:T(8,128)(2,1)}), bf16[16,256,256]{2,1,0:T(8,128)(2,1)}, u32[]{:S(2)}, u32[]{:S(2)}) %all-to-all-start) | async-done | bytes 2097184 | tf_op jit(solution)/shard_map/all_to_all | solution.py:402
  326.0 8.7 %turn.4.refs_0_ = bf16[128,64,128]{2,1,0:T(8,128)(2,1)} custom-call(bf16[16,256,256]{2,1,0:T(8,128)(2,1)} %all-to-all-done.in_ref), custom_call_target="tpu_custom_call" | custom-call | flops 4194304 | bytes 4194304 | tf_op jit(solution)/shard_map/turn/pallas_call | solution.py:319
  334.7 37.1 %correlate.1 = f32[8,16,256,256]{3,2,1,0:T(8,128)} custom-call(s32[16]{0:T(128)} %compare_select_fusion.3.order_ref, bf16[128,64,128]{2,1,0:T(8,128)(2,1)} %turn.4.refs_0_, bf16[128,64,128]{2,1,0:T(8,128)(2,1)} %turn.5.refs_1_, bf16[128,64,128]{2,1,0:T(8,128)(2,1)} %turn.6.refs_2_, bf16[128,64,128]{2,1,0:T(8,128)(2,1)} %turn.7.refs_3_), custom_call_target="tpu_custom_call" | custom-call | flops 4294967296 | bytes 41943040 | tf_op jit(solution)/shard_map/correlate/pallas_call | solution.py:363
Async XLA Ops:
  5.7 6.2 %collective-permute-start.3 = (bf16[16,16,4096]{2,1,0:T(8,128)(2,1)S(1)}, bf16[16,16,4096]{2,1,0:T(8,128)(2,1)S(1)}, u32[]{:S(2)}, u32[]{:S(2)}) collective-permute-start(bf16[16,16,4096]{2,1,0:T(8,128)(2,1)S(1)} %get-tuple-element.5), channel_id=1, source_target_pairs={{0,1},{1,2},{2,3},{4,5},{5,6},{6,7},{8,9},{9,10},{10,11},{12,13},{... | collective-permute-start | bytes 6291464 | tf_op jit(solution)/shard_map/ppermute | solution.py:23
  11.9 1.4 copy-start.3
  32.1 75.1 %all-to-all-start.3 = ((bf16[16,256,256]{2,1,0:T(8,128)(2,1)}), bf16[16,256,256]{2,1,0:T(8,128)(2,1)S(1)}, u32[]{:S(2)}, u32[]{:S(2)}) async-start(bf16[16,256,256]{2,1,0:T(8,128)(2,1)} %filter_bank.7), calls=%async_computation.3 | async-start | bytes 4194304 | tf_op jit(solution)/shard_map/all_to_all | solution.py:402
  59.8 6.3 %collective-permute-start.2 = (bf16[16,16,4096]{2,1,0:T(8,128)(2,1)}, bf16[16,16,4096]{2,1,0:T(8,128)(2,1)S(1)}, u32[]{:S(2)}, u32[]{:S(2)}) collective-permute-start(bf16[16,16,4096]{2,1,0:T(8,128)(2,1)} %get-tuple-element.6), channel_id=1, source_target_pairs={{0,1},{1,2},{2,3},{4,5},{5,6},{6,7},{8,9},{9,10},{10,11},{12,13},{... | collective-permute-start | bytes 6291464 | tf_op jit(solution)/shard_map/ppermute | solution.py:23
  66.0 1.3 copy-start.4
  107.2 1.4 copy-start
  108.6 72.1 %all-to-all-start.2 = ((bf16[16,256,256]{2,1,0:T(8,128)(2,1)}), bf16[16,256,256]{2,1,0:T(8,128)(2,1)}, u32[]{:S(2)}, u32[]{:S(2)}) async-start(bf16[16,256,256]{2,1,0:T(8,128)(2,1)} %filter_bank.6), calls=%async_computation.2 | async-start | bytes 4194304 | tf_op jit(solution)/shard_map/all_to_all | solution.py:402
  133.2 6.3 %collective-permute-start.1 = (bf16[16,16,4096]{2,1,0:T(8,128)(2,1)}, bf16[16,16,4096]{2,1,0:T(8,128)(2,1)S(1)}, u32[]{:S(2)}, u32[]{:S(2)}) collective-permute-start(bf16[16,16,4096]{2,1,0:T(8,128)(2,1)} %get-tuple-element.7), channel_id=1, source_target_pairs={{0,1},{1,2},{2,3},{4,5},{5,6},{6,7},{8,9},{9,10},{10,11},{12,13},{... | collective-permute-start | bytes 6291464 | tf_op jit(solution)/shard_map/ppermute | solution.py:23
  139.4 1.3 copy-start.5
  180.7 71.9 %all-to-all-start.1 = ((bf16[16,256,256]{2,1,0:T(8,128)(2,1)}), bf16[16,256,256]{2,1,0:T(8,128)(2,1)S(1)}, u32[]{:S(2)}, u32[]{:S(2)}) async-start(bf16[16,256,256]{2,1,0:T(8,128)(2,1)} %filter_bank.5), calls=%async_computation.1 | async-start | bytes 4194304 | tf_op jit(solution)/shard_map/all_to_all | solution.py:402
  205.2 6.3 %collective-permute-start = (bf16[16,16,4096]{2,1,0:T(8,128)(2,1)}, bf16[16,16,4096]{2,1,0:T(8,128)(2,1)S(1)}, u32[]{:S(2)}, u32[]{:S(2)}) collective-permute-start(bf16[16,16,4096]{2,1,0:T(8,128)(2,1)} %get-tuple-element.8), channel_id=1, source_target_pairs={{0,1},{1,2},{2,3},{4,5},{5,6},{6,7},{8,9},{9,10},{10,11},{12,13},{... | collective-permute-start | bytes 6291464 | tf_op jit(solution)/shard_map/ppermute | solution.py:23
  211.4 1.3 copy-start.2
  252.6 1.3 copy-start.1
  253.9 72.1 %all-to-all-start = ((bf16[16,256,256]{2,1,0:T(8,128)(2,1)}), bf16[16,256,256]{2,1,0:T(8,128)(2,1)}, u32[]{:S(2)}, u32[]{:S(2)}) async-start(bf16[16,256,256]{2,1,0:T(8,128)(2,1)} %filter_bank.4), calls=%async_computation | async-start | bytes 4194304 | tf_op jit(solution)/shard_map/all_to_all | solution.py:402

commit v2 on v1

--- a/solution.py
+++ b/solution.py
@@ -240,7 +240,7 @@
             spec_ref[group] = total
             return carry
 
-        lax.fori_loop(0, GROUPS, one_group, 0)
+        lax.fori_loop(0, GROUPS, one_group, 0, unroll=GROUPS)
         owners = out_ref.shape[0]
         slots = GROUPS
         run = LANES // slots
@@ -308,7 +308,7 @@
         work_ref[pl.ds(i, LANES, stride=count), :] = square.T
         return carry
 
-    lax.fori_loop(0, count, one_input, 0)
+    lax.fori_loop(0, count, one_input, 0, unroll=8)
     out_ref[...] = work_ref[...].reshape(LANES, count, LANES).astype(jnp.bfloat16)
 
 
@@ -323,7 +323,7 @@
         in_specs=[pl.BlockSpec((blocks, rows, 2 * LANES), lambda z: (z, 0, 0))],
         out_specs=pl.BlockSpec((LANES, count, LANES), lambda z: (0, z, 0)),
         scratch_shapes=[pltpu.VMEM((LANES * count, LANES), jnp.float32)],
-        compiler_params=pltpu.CompilerParams(vmem_limit_bytes=56 * MIB),
+        compiler_params=pltpu.CompilerParams(vmem_limit_bytes=20 * MIB),
         cost_estimate=pl.CostEstimate(flops=4 * arrived.size, bytes_accessed=4 * arrived.size, transcendentals=0),
         name="turn",
     )(arrived)
@@ -342,18 +342,20 @@
             ],
             axis=0,
         )
-        lane = lax.broadcasted_iota(jnp.int32, joined.shape, 1)
-        wide = pltpu.roll(joined.astype(jnp.float32), LANES // 2, 1)
-        turned = jnp.where(lane < LANES // 2, wide, -wide).astype(jnp.bfloat16)
-        across = (((1,), (1,)), ((), ()))
-        real = lax.dot_general(joined, joined, across, preferred_element_type=jnp.float32)
-        imag = lax.dot_general(turned, joined, across, preferred_element_type=jnp.float32)
+        turned = jnp.concatenate([joined[:, LANES // 2 :], -joined[:, : LANES // 2]], axis=1)
+        both = lax.dot_general(
+            jnp.concatenate([joined, turned], axis=0),
+            joined,
+            (((1,), (1,)), ((), ())),
+            preferred_element_type=jnp.float32,
+        )
+        real, imag = both[: joined.shape[0]], both[joined.shape[0] :]
         row = lax.broadcasted_iota(jnp.int32, real.shape, 0)
         col = lax.broadcasted_iota(jnp.int32, real.shape, 1)
         out_ref[u, 0] = jnp.where(row <= col, real, imag) * scale
         return carry
 
-    lax.fori_loop(0, held, one_channel, 0)
+    lax.fori_loop(0, held, one_channel, 0, unroll=held)
 
 
 def correlate_all(turned, counts, sets, order, scale):
@@ -369,7 +371,7 @@
             in_specs=[pl.BlockSpec((held, sets * count, LANES), lambda s, order: (s, 0, 0)) for count in counts],
             out_specs=pl.BlockSpec((held, 1, width, width), lambda s, order: (0, order[s], 0, 0)),
         ),
-        compiler_params=pltpu.CompilerParams(vmem_limit_bytes=56 * MIB),
+        compiler_params=pltpu.CompilerParams(vmem_limit_bytes=24 * MIB),
         cost_estimate=pl.CostEstimate(
             flops=4 * channels * width * width * LANES, bytes_accessed=40 * MIB, transcendentals=0
         ),
@@ -395,10 +397,15 @@
     steps = jnp.arange(RADIX, dtype=jnp.int32)
     group, side = (slot - steps // 2) % GROUPS, steps % 2
     order = jnp.where(group == 0, side * GROUPS, jnp.where(side == 0, group, RADIX - group)).astype(jnp.int32)
+    histories, source = [], samples
+    for first, count in zip(starts, counts):
+        histories.append(from_behind(source[first : first + count], ("tm", "pol"), 1))
+        source, histories[-1] = lax.optimization_barrier((source, histories[-1]))
     turned = []
-    for first, count in zip(starts, counts):
-        history = from_behind(samples[first : first + count], ("tm", "pol"), 1)
-        spectra = filter_bank(samples, history, coefficients, table, first, count, owners)
+    for k, (first, count) in enumerate(zip(starts, counts)):
+        spectra = filter_bank(samples, histories[k], coefficients, table, first, count, owners)
+        if k + 1 < len(counts):
+            spectra, histories[k + 1] = lax.optimization_barrier((spectra, histories[k + 1]))
         arrived = lax.all_to_all(spectra, everyone, 0, 0, tiled=True)
         turned.append(turn(arrived, sets, frames))
     return correlate_all(turned, counts, sets, order, 1.0 / total_frames)

time: 372 us -> 295 us (0.79)
  starting transfers between devices: 106 us -> 47.8 us
  Pallas kernels: 147 us -> 100 us
  waiting for transfers between devices: 104 us -> 132 us
    all_to_all x4, starting transfers between devices: 101 us -> 42.7 us  [fast(): arrived = lax.all_to_all(spectra, everyone, 0, 0, tiled=True)]
    all_to_all x4, waiting for transfers between devices: 83.9 us -> 118 us  [fast(): arrived = lax.all_to_all(spectra, everyone, 0, 0, tiled=True)]
    pallas_call x4, Pallas kernels: 34.8 us -> 12.2 us  [turn(): pl.pallas_call(functools.partial(turn_kernel, frames), out_shape=jax.Shap...]
    pallas_call x1, Pallas kernels: 37.1 us -> 17.6 us  [correlate_all(): pl.pallas_call(functools.partial(correlate_kernel, counts, sets, scale),...]
    ppermute x4, waiting for transfers between devices: 19.8 us -> 13.4 us  [from_behind(): return lax.ppermute(block, axis, route)]
    pallas_call x4, Pallas kernels: 75.3 us -> 70.7 us  [filter_bank(): pl.pallas_call(functools.partial(filter_bank_kernel, steps), out_shape=ja...]
    slice x1 -> x4, local copies, waits for them, and re-layouts: 5.68 us -> 7.88 us  [fast(): histories.append(from_behind(source[first:first + count], ('tm', 'pol'), 1))]
    unnamed x12 -> x18, local copies, waits for them, and re-layouts: 8 us -> 6.92 us
  transfers between devices with their start and end apart: 8 -> 8, of which waited for: 8 -> 6; matrix products, arithmetic and copies ran while one was open for 0% -> 1% of each run, Pallas kernels for 22% -> 27%
where the time goes in v2:
time: 295 us
  waiting for transfers between devices  132 us (45%)
  Pallas kernels  100 us (34%)
  starting transfers between devices  47.8 us (16%)
  local copies, waits for them, and re-layouts  14.8 us (5%)
    all_to_all x4, waiting for transfers between devices, fast(): arrived = lax.all_to_all(spectra, everyone, 0, 0, tiled=True)  118 us
    pallas_call x4, Pallas kernels, filter_bank(): pl.pallas_call(functools.partial(filter_bank_kernel, steps), out_shape=ja...  70.7 us
    all_to_all x4, starting transfers between devices, fast(): arrived = lax.all_to_all(spectra, everyone, 0, 0, tiled=True)  42.7 us
    pallas_call x1, Pallas kernels, correlate_all(): pl.pallas_call(functools.partial(correlate_kernel, counts, sets, scale),...  17.6 us
    ppermute x4, waiting for transfers between devices, from_behind(): return lax.ppermute(block, axis, route)  13.4 us
    pallas_call x4, Pallas kernels, turn(): pl.pallas_call(functools.partial(turn_kernel, frames), out_shape=jax.Shap...  12.2 us
    slice x4, local copies, waits for them, and re-layouts, fast(): histories.append(from_behind(source[first:first + count], ('tm', 'pol'), 1))  7.88 us
    unnamed x18, local copies, waits for them, and re-layouts  6.92 us
  transfers between devices with their start and end apart: 8, of which 6 were waited for; matrix products, arithmetic and copies ran while one was open for 1% of the time, Pallas kernels for 27%

profile of v2, /device:TPU:15, one launch (start us, length us, event | category | flops | bytes accessed | tf_op | source)
XLA Modules:
  0.0 294.8 jit_solution(15154192982107847315)
XLA Ops:
  0.0 1.7 slice.12
  1.7 1.3 collective-permute-start
  3.0 4.9 %collective-permute-done.old_ref = bf16[16,16,4096]{2,1,0:T(8,128)(2,1)S(1)} collective-permute-done((bf16[16,16,4096]{2,1,0:T(8,128)(2,1)S(1)}, bf16[16,16,4096]{2,1,0:T(8,128)(2,1)S(1)}, u32[]{:S(2)}, u32[]{:S(2)}) %collective-permute-start) | collective-permute-done | bytes 2097184 | tf_op jit(solution)/shard_map/ppermute | solution.py:23
  8.0 0.0 copy-start.8
  8.0 2.6 slice.13
  10.5 0.0 copy-done.8
  10.5 1.3 collective-permute-start.1
  11.8 17.7 %filter_bank.4 = bf16[16,256,256]{2,1,0:T(8,128)(2,1)} custom-call(bf16[64,16,4096]{2,1,0:T(8,128)(2,1)} %own_ref.7, bf16[16,16,4096]{2,1,0:T(8,128)(2,1)} %copy-done.8, f32[16,4096]{1,0:T(8,128)} %coef_ref.7, bf16[8,2,512,512]{3,2,1,0:T(8,128)(2,1)} %constant.65.clone.table_hbm), custom_call_target="tpu_custom_call" | custom-call | flops 1610612736 | bytes 16777216 | tf_op jit(solution)/shard_map/filter_bank/pallas_call | solution.py:270
  29.5 8.5 %collective-permute-done.1.old_ref = bf16[16,16,4096]{2,1,0:T(8,128)(2,1)} collective-permute-done((bf16[16,16,4096]{2,1,0:T(8,128)(2,1)S(1)}, bf16[16,16,4096]{2,1,0:T(8,128)(2,1)}, u32[]{:S(2)}, u32[]{:S(2)}) %collective-permute-start.1) | collective-permute-done | bytes 2097184 | tf_op jit(solution)/shard_map/ppermute | solution.py:23
  38.0 27.7 %all-to-all-start = ((bf16[16,256,256]{2,1,0:T(8,128)(2,1)}), bf16[16,256,256]{2,1,0:T(8,128)(2,1)S(1)}, u32[]{:S(2)}, u32[]{:S(2)}) async-start(bf16[16,256,256]{2,1,0:T(8,128)(2,1)} %filter_bank.4), calls=%async_computation | async-start | bytes 4194304 | tf_op jit(solution)/shard_map/all_to_all | solution.py:409
  65.7 1.8 slice.14
  67.5 1.3 collective-permute-start.2
  68.8 17.7 %filter_bank.5 = bf16[16,256,256]{2,1,0:T(8,128)(2,1)} custom-call(bf16[64,16,4096]{2,1,0:T(8,128)(2,1)} %own_ref.7, bf16[16,16,4096]{2,1,0:T(8,128)(2,1)} %collective-permute-done.1.old_ref, f32[16,4096]{1,0:T(8,128)} %coef_ref.7, bf16[8,2,512,512]{3,2,1,0:T(8,128)(2,1)} %constant.65.clone.table_hbm), custom_call_target="tpu_custom_call" | custom-call | flops 1610612736 | bytes 16777216 | tf_op jit(solution)/shard_map/filter_bank/pallas_call | solution.py:270
  86.4 0.0 collective-permute-done.2.old_ref
  86.5 26.6 %all-to-all-done.in_ref = bf16[16,256,256]{2,1,0:T(8,128)(2,1)S(1)} async-done(((bf16[16,256,256]{2,1,0:T(8,128)(2,1)}), bf16[16,256,256]{2,1,0:T(8,128)(2,1)S(1)}, u32[]{:S(2)}, u32[]{:S(2)}) %all-to-all-start) | async-done | bytes 2097184 | tf_op jit(solution)/shard_map/all_to_all | solution.py:409
  113.1 0.0 copy-start.4
  113.1 1.3 copy-done.4
  114.4 5.0 %all-to-all-start.1 = ((bf16[16,256,256]{2,1,0:T(8,128)(2,1)}), bf16[16,256,256]{2,1,0:T(8,128)(2,1)}, u32[]{:S(2)}, u32[]{:S(2)}) async-start(bf16[16,256,256]{2,1,0:T(8,128)(2,1)} %filter_bank.5), calls=%async_computation.1 | async-start | bytes 4194304 | tf_op jit(solution)/shard_map/all_to_all | solution.py:409
  119.5 1.8 slice.15
  121.3 1.3 collective-permute-start.3
  122.6 17.7 %filter_bank.6 = bf16[16,256,256]{2,1,0:T(8,128)(2,1)} custom-call(bf16[64,16,4096]{2,1,0:T(8,128)(2,1)} %own_ref.7, bf16[16,16,4096]{2,1,0:T(8,128)(2,1)} %collective-permute-done.2.old_ref, f32[16,4096]{1,0:T(8,128)} %coef_ref.7, bf16[8,2,512,512]{3,2,1,0:T(8,128)(2,1)} %constant.65.clone.table_hbm), custom_call_target="tpu_custom_call" | custom-call | flops 1610612736 | bytes 16777216 | tf_op jit(solution)/shard_map/filter_bank/pallas_call | solution.py:270
  140.3 0.0 collective-permute-done.3.old_ref
  140.3 26.7 %all-to-all-done.1.in_ref = bf16[16,256,256]{2,1,0:T(8,128)(2,1)} async-done(((bf16[16,256,256]{2,1,0:T(8,128)(2,1)}), bf16[16,256,256]{2,1,0:T(8,128)(2,1)}, u32[]{:S(2)}, u32[]{:S(2)}) %all-to-all-start.1) | async-done | bytes 2097184 | tf_op jit(solution)/shard_map/all_to_all | solution.py:409
  167.0 5.0 %all-to-all-start.2 = ((bf16[16,256,256]{2,1,0:T(8,128)(2,1)}), bf16[16,256,256]{2,1,0:T(8,128)(2,1)S(1)}, u32[]{:S(2)}, u32[]{:S(2)}) async-start(bf16[16,256,256]{2,1,0:T(8,128)(2,1)} %filter_bank.6), calls=%async_computation.2 | async-start | bytes 4194304 | tf_op jit(solution)/shard_map/all_to_all | solution.py:409
  172.0 17.6 %filter_bank.7 = bf16[16,256,256]{2,1,0:T(8,128)(2,1)} custom-call(bf16[64,16,4096]{2,1,0:T(8,128)(2,1)} %own_ref.7, bf16[16,16,4096]{2,1,0:T(8,128)(2,1)} %collective-permute-done.3.old_ref, f32[16,4096]{1,0:T(8,128)} %coef_ref.7, bf16[8,2,512,512]{3,2,1,0:T(8,128)(2,1)} %constant.65.clone.table_hbm), custom_call_target="tpu_custom_call" | custom-call | flops 1610612736 | bytes 16777216 | tf_op jit(solution)/shard_map/filter_bank/pallas_call | solution.py:270
  189.7 29.8 %all-to-all-done.2.in_ref = bf16[16,256,256]{2,1,0:T(8,128)(2,1)S(1)} async-done(((bf16[16,256,256]{2,1,0:T(8,128)(2,1)}), bf16[16,256,256]{2,1,0:T(8,128)(2,1)S(1)}, u32[]{:S(2)}, u32[]{:S(2)}) %all-to-all-start.2) | async-done | bytes 2097184 | tf_op jit(solution)/shard_map/all_to_all | solution.py:409
  219.4 0.0 copy-start.6
  219.5 1.4 copy-done.6
  220.8 4.9 %all-to-all-start.3 = ((bf16[16,256,256]{2,1,0:T(8,128)(2,1)}), bf16[16,256,256]{2,1,0:T(8,128)(2,1)}, u32[]{:S(2)}, u32[]{:S(2)}) async-start(bf16[16,256,256]{2,1,0:T(8,128)(2,1)} %filter_bank.7), calls=%async_computation.3 | async-start | bytes 4194304 | tf_op jit(solution)/shard_map/all_to_all | solution.py:409
  225.7 0.0 copy-start.5
  225.7 1.6 copy-done.5
  227.3 2.2 turn.4.refs_0_
  229.5 0.0 copy-start.7
  229.5 3.9 %turn.5.refs_1_ = bf16[128,64,128]{2,1,0:T(8,128)(2,1)S(1)} custom-call(bf16[16,256,256]{2,1,0:T(8,128)(2,1)} %all-to-all-done.1.in_ref), custom_call_target="tpu_custom_call" | custom-call | flops 4194304 | bytes 4194304 | tf_op jit(solution)/shard_map/turn/pallas_call | solution.py:319
  233.4 0.0 copy-start
  233.4 1.3 copy-done
  234.8 0.0 copy-done.7
  234.8 2.2 turn.6.refs_2_
  236.9 0.0 copy-start.2
  236.9 1.3 copy-done.2
  238.3 35.0 %all-to-all-done.3.in_ref = bf16[16,256,256]{2,1,0:T(8,128)(2,1)} async-done(((bf16[16,256,256]{2,1,0:T(8,128)(2,1)}), bf16[16,256,256]{2,1,0:T(8,128)(2,1)}, u32[]{:S(2)}, u32[]{:S(2)}) %all-to-all-start.3) | async-done | bytes 2097184 | tf_op jit(solution)/shard_map/all_to_all | solution.py:409
  273.2 0.0 copy-start.1
  273.2 0.0 copy-start.3
  273.2 3.9 %turn.7.refs_3_ = bf16[128,64,128]{2,1,0:T(8,128)(2,1)S(1)} custom-call(bf16[16,256,256]{2,1,0:T(8,128)(2,1)} %all-to-all-done.3.in_ref), custom_call_target="tpu_custom_call" | custom-call | flops 4194304 | bytes 4194304 | tf_op jit(solution)/shard_map/turn/pallas_call | solution.py:319
  277.2 0.0 copy-done.1
  277.2 0.0 copy-done.3
  277.2 17.6 %correlate.1 = f32[8,16,256,256]{3,2,1,0:T(8,128)} custom-call(s32[16]{0:T(128)S(1)} %compare_select_fusion.3.order_ref, bf16[128,64,128]{2,1,0:T(8,128)(2,1)S(1)} %turn.4.refs_0_, bf16[128,64,128]{2,1,0:T(8,128)(2,1)S(1)} %copy-done.1, bf16[128,64,128]{2,1,0:T(8,128)(2,1)S(1)} %copy-done.3, bf16[128,64,128]{2,1,0:T(8,128)(2,1)S(1)} %turn.7.refs_3_), custom_call_target="tpu_custom_call" | custom-call | flops 4294967296 | bytes 41943040 | tf_op jit(solution)/shard_map/correlate/pallas_call | solution.py:365
  (1 shorter events, 0.0 us)
Async XLA Ops:
  1.7 6.2 %collective-permute-start = (bf16[16,16,4096]{2,1,0:T(8,128)(2,1)S(1)}, bf16[16,16,4096]{2,1,0:T(8,128)(2,1)S(1)}, u32[]{:S(2)}, u32[]{:S(2)}) collective-permute-start(bf16[16,16,4096]{2,1,0:T(8,128)(2,1)S(1)} %slice.12), channel_id=1, source_target_pairs={{0,1},{1,2},{2,3},{4,5},{5,6},{6,7},{8,9},{9,10},{10,11},{12,13},{... | collective-permute-start | bytes 6291464 | tf_op jit(solution)/shard_map/ppermute | solution.py:23
  8.0 2.6 copy-start.8
  10.5 27.5 %collective-permute-start.1 = (bf16[16,16,4096]{2,1,0:T(8,128)(2,1)S(1)}, bf16[16,16,4096]{2,1,0:T(8,128)(2,1)}, u32[]{:S(2)}, u32[]{:S(2)}) collective-permute-start(bf16[16,16,4096]{2,1,0:T(8,128)(2,1)S(1)} %slice.13), channel_id=1, source_target_pairs={{0,1},{1,2},{2,3},{4,5},{5,6},{6,7},{8,9},{9,10},{10,11},{12,13},{... | collective-permute-start | bytes 6291464 | tf_op jit(solution)/shard_map/ppermute | solution.py:23
  38.0 75.1 %all-to-all-start = ((bf16[16,256,256]{2,1,0:T(8,128)(2,1)}), bf16[16,256,256]{2,1,0:T(8,128)(2,1)S(1)}, u32[]{:S(2)}, u32[]{:S(2)}) async-start(bf16[16,256,256]{2,1,0:T(8,128)(2,1)} %filter_bank.4), calls=%async_computation | async-start | bytes 4194304 | tf_op jit(solution)/shard_map/all_to_all | solution.py:409
  67.5 19.0 %collective-permute-start.2 = (bf16[16,16,4096]{2,1,0:T(8,128)(2,1)S(1)}, bf16[16,16,4096]{2,1,0:T(8,128)(2,1)}, u32[]{:S(2)}, u32[]{:S(2)}) collective-permute-start(bf16[16,16,4096]{2,1,0:T(8,128)(2,1)S(1)} %slice.14), channel_id=1, source_target_pairs={{0,1},{1,2},{2,3},{4,5},{5,6},{6,7},{8,9},{9,10},{10,11},{12,13},{... | collective-permute-start | bytes 6291464 | tf_op jit(solution)/shard_map/ppermute | solution.py:23
  113.1 1.3 copy-start.4
  114.4 52.6 %all-to-all-start.1 = ((bf16[16,256,256]{2,1,0:T(8,128)(2,1)}), bf16[16,256,256]{2,1,0:T(8,128)(2,1)}, u32[]{:S(2)}, u32[]{:S(2)}) async-start(bf16[16,256,256]{2,1,0:T(8,128)(2,1)} %filter_bank.5), calls=%async_computation.1 | async-start | bytes 4194304 | tf_op jit(solution)/shard_map/all_to_all | solution.py:409
  121.3 19.0 %collective-permute-start.3 = (bf16[16,16,4096]{2,1,0:T(8,128)(2,1)S(1)}, bf16[16,16,4096]{2,1,0:T(8,128)(2,1)}, u32[]{:S(2)}, u32[]{:S(2)}) collective-permute-start(bf16[16,16,4096]{2,1,0:T(8,128)(2,1)S(1)} %slice.15), channel_id=1, source_target_pairs={{0,1},{1,2},{2,3},{4,5},{5,6},{6,7},{8,9},{9,10},{10,11},{12,13},{... | collective-permute-start | bytes 6291464 | tf_op jit(solution)/shard_map/ppermute | solution.py:23
  167.0 52.5 %all-to-all-start.2 = ((bf16[16,256,256]{2,1,0:T(8,128)(2,1)}), bf16[16,256,256]{2,1,0:T(8,128)(2,1)S(1)}, u32[]{:S(2)}, u32[]{:S(2)}) async-start(bf16[16,256,256]{2,1,0:T(8,128)(2,1)} %filter_bank.6), calls=%async_computation.2 | async-start | bytes 4194304 | tf_op jit(solution)/shard_map/all_to_all | solution.py:409
  219.4 1.4 copy-start.6
  220.8 52.4 %all-to-all-start.3 = ((bf16[16,256,256]{2,1,0:T(8,128)(2,1)}), bf16[16,256,256]{2,1,0:T(8,128)(2,1)}, u32[]{:S(2)}, u32[]{:S(2)}) async-start(bf16[16,256,256]{2,1,0:T(8,128)(2,1)} %filter_bank.7), calls=%async_computation.3 | async-start | bytes 4194304 | tf_op jit(solution)/shard_map/all_to_all | solution.py:409
  225.7 1.6 copy-start.5
  229.5 5.3 %copy-start.7 = (bf16[16,256,256]{2,1,0:T(8,128)(2,1)S(1)}, bf16[16,256,256]{2,1,0:T(8,128)(2,1)}, u32[]{:S(2)}) copy-start(bf16[16,256,256]{2,1,0:T(8,128)(2,1)} %copy-done.6) | copy-start | bytes 6291460
  233.4 1.3 copy-start
  236.9 1.3 copy-start.2
  273.2 3.9 %copy-start.1 = (bf16[128,64,128]{2,1,0:T(8,128)(2,1)S(1)}, bf16[128,64,128]{2,1,0:T(8,128)(2,1)}, u32[]{:S(2)}) copy-start(bf16[128,64,128]{2,1,0:T(8,128)(2,1)} %copy-done) | copy-start | bytes 6291460
  273.2 3.9 %copy-start.3 = (bf16[128,64,128]{2,1,0:T(8,128)(2,1)S(1)}, bf16[128,64,128]{2,1,0:T(8,128)(2,1)}, u32[]{:S(2)}) copy-start(bf16[128,64,128]{2,1,0:T(8,128)(2,1)} %copy-done.2) | copy-start | bytes 6291460

commit v3 on v2

--- a/solution.py
+++ b/solution.py
@@ -176,26 +176,41 @@
     return bins
 
 
-def filter_bank_kernel(
-    steps, own_ref, old_ref, coef_ref, table_hbm, out_ref, frames_ref, kept_ref, high_ref, low_ref, spec_ref, table_ref, sem
-):
+def filter_bank_kernel(steps, following, own_ref, coef_ref, table_hbm, history_hbm, *refs):
+    if following:
+        samples_hbm, out_ref, piece_hbm, *refs, piece_ref = refs
+        fetch = pltpu.make_async_copy(samples_hbm.at[pl.ds(*following)], piece_ref, refs[-1].at[steps + 1])
+        store = pltpu.make_async_copy(piece_ref, piece_hbm, refs[-1].at[steps + 2])
+    else:
+        out_ref, *refs = refs
+    past_ref, frames_ref, kept_ref, high_ref, low_ref, spec_ref, table_ref, sems = refs
     inputs, frames, length = own_ref.shape
     taps = coef_ref.shape[0]
     span = length // RADIX
     parts = span // LANES
     step = pl.program_id(0)
-    copy = pltpu.make_async_copy(table_hbm, table_ref, sem)
+    copy = pltpu.make_async_copy(table_hbm, table_ref, sems.at[steps])
 
     @pl.when(step == 0)
     def _():
+        for k in range(steps):
+            pltpu.make_async_copy(history_hbm.at[pl.ds(k * inputs, inputs)], past_ref.at[k], sems.at[k]).start()
         copy.start()
+        if following:
+            fetch.start()
+
+    for k in range(steps):
+
+        @pl.when(step == k)
+        def _():
+            pltpu.make_async_copy(history_hbm.at[pl.ds(k * inputs, inputs)], past_ref.at[k], sems.at[k]).wait()
 
     base = step * inputs * frames
 
     def one_block(block, carry):
         lanes = pl.ds(pl.multiple_of(block * LANES, LANES), LANES)
         for i in range(inputs):
-            frames_ref[pl.ds(2 * frames * i, frames), :] = old_ref[i, :, lanes].astype(jnp.float32)
+            frames_ref[pl.ds(2 * frames * i, frames), :] = past_ref[step, i, :, lanes].astype(jnp.float32)
             frames_ref[pl.ds(2 * frames * i + frames, frames), :] = own_ref[i, :, lanes].astype(jnp.float32)
         taps_now = [jnp.broadcast_to(coef_ref[t : t + 1, lanes], (ROWS, LANES)) for t in range(taps)]
         first = frames - taps + 1
@@ -210,6 +225,13 @@
         return carry
 
     lax.fori_loop(0, length // LANES, one_block, 0)
+    if following:
+
+        @pl.when(step == 0)
+        def _():
+            fetch.wait()
+            store.start()
+
 
     def one_rows(index, carry):
         part = index % parts
@@ -260,37 +282,67 @@
             return carry
 
         lax.fori_loop(0, out_ref.shape[1] // 16, one_part, 0)
-
-
-def filter_bank(samples, history, coefficients, table, first, count, owners):
+        if following:
+            store.wait()
+
+
+def filter_bank(samples, history, coefficients, table, first, count, owners, following):
     _, frames, length = samples.shape
     steps = count // ROWS
     rows = count * frames
     offset = first // ROWS
+    in_specs = [
+        pl.BlockSpec((ROWS, frames, length), lambda i: (i + offset, 0, 0)),
+        pl.BlockSpec(coefficients.shape, lambda i: (0, 0), pipeline_mode=pl.Buffered(1)),
+        pl.BlockSpec(memory_space=pl.ANY),
+        pl.BlockSpec(memory_space=pl.ANY),
+    ]
+    out_specs = [pl.BlockSpec((owners, rows, 2 * LANES), lambda i: (0, 0, 0), pipeline_mode=pl.Buffered(1))]
+    out_shape = [jax.ShapeDtypeStruct((owners, rows, 2 * LANES), jnp.bfloat16)]
+    operands = [samples, coefficients, table, history]
+    if following:
+        in_specs.append(pl.BlockSpec(memory_space=pl.ANY))
+        out_specs.append(pl.BlockSpec(memory_space=pl.ANY))
+        out_shape.append(jax.ShapeDtypeStruct((following[1], frames, length), samples.dtype))
+        operands.append(samples)
     return pl.pallas_call(
-        functools.partial(filter_bank_kernel, steps),
-        out_shape=jax.ShapeDtypeStruct((owners, rows, 2 * LANES), jnp.bfloat16),
+        functools.partial(filter_bank_kernel, steps, following),
+        out_shape=out_shape,
         grid=(steps,),
-        in_specs=[
-            pl.BlockSpec((ROWS, frames, length), lambda i: (i + offset, 0, 0)),
-            pl.BlockSpec((ROWS, frames, length), lambda i: (i, 0, 0)),
-            pl.BlockSpec(coefficients.shape, lambda i: (0, 0), pipeline_mode=pl.Buffered(1)),
-            pl.BlockSpec(memory_space=pl.ANY),
-        ],
-        out_specs=pl.BlockSpec((owners, rows, 2 * LANES), lambda i: (0, 0, 0), pipeline_mode=pl.Buffered(1)),
+        in_specs=in_specs,
+        out_specs=out_specs,
         scratch_shapes=[
+            pltpu.VMEM((steps, ROWS, frames, length), jnp.bfloat16),
             pltpu.VMEM((2 * ROWS * frames, LANES), jnp.float32),
             pltpu.VMEM((length // LANES, ROWS * frames, LANES), jnp.float32),
             pltpu.VMEM((GROUPS, rows, 2 * length // RADIX), jnp.bfloat16),
             pltpu.VMEM((GROUPS, rows, 2 * length // RADIX), jnp.bfloat16),
             pltpu.VMEM((GROUPS, rows, 2 * owners * LANES // GROUPS), jnp.float32),
             pltpu.VMEM(table.shape, jnp.bfloat16),
-            pltpu.SemaphoreType.DMA,
-        ],
-        compiler_params=pltpu.CompilerParams(vmem_limit_bytes=56 * MIB),
-        cost_estimate=pl.CostEstimate(flops=rows * length * 512 * 3, bytes_accessed=16 * MIB, transcendentals=0),
+            pltpu.SemaphoreType.DMA((steps + 3,)),
+        ]
+        + ([pltpu.VMEM((following[1], frames, length), samples.dtype)] if following else []),
+        compiler_params=pltpu.CompilerParams(vmem_limit_bytes=62 * MIB),
+        cost_estimate=pl.CostEstimate(flops=10**11, bytes_accessed=16 * MIB, transcendentals=0),
         name="filter_bank",
-    )(samples, history, coefficients, table)
+    )(*operands)
+
+
+def cut_kernel(in_ref, out_ref):
+    out_ref[...] = in_ref[...]
+
+
+def cut(samples, first, count):
+    block = (ROWS, *samples.shape[1:])
+    return pl.pallas_call(
+        cut_kernel,
+        out_shape=jax.ShapeDtypeStruct((count, *samples.shape[1:]), samples.dtype),
+        grid=(count // ROWS,),
+        in_specs=[pl.BlockSpec(block, lambda i: (i + first // ROWS, 0, 0))],
+        out_specs=pl.BlockSpec(block, lambda i: (i, 0, 0)),
+        cost_estimate=pl.CostEstimate(flops=0, bytes_accessed=4 * MIB, transcendentals=0),
+        name="cut",
+    )(samples)
 
 
 def turn_kernel(frames, in_ref, out_ref, work_ref):
@@ -381,7 +433,8 @@
 
 
 def plan(in_dev):
-    return [in_dev // 4] * 4
+    units = in_dev // ROWS
+    return [ROWS * size for size in (1, 2, 2, units - 5)]
 
 
 def fast(samples, coefficients):
@@ -397,17 +450,27 @@
     steps = jnp.arange(RADIX, dtype=jnp.int32)
     group, side = (slot - steps // 2) % GROUPS, steps % 2
     order = jnp.where(group == 0, side * GROUPS, jnp.where(side == 0, group, RADIX - group)).astype(jnp.int32)
-    histories, source = [], samples
-    for first, count in zip(starts, counts):
-        histories.append(from_behind(source[first : first + count], ("tm", "pol"), 1))
-        source, histories[-1] = lax.optimization_barrier((source, histories[-1]))
+    last = len(counts) - 1
+    parts = list(zip(starts, counts))
+    histories = [from_behind(samples[: counts[0]], ("tm", "pol"), 1)]
+    piece, histories[0] = lax.optimization_barrier((cut(samples, *parts[1]), histories[0]))
+    histories.append(from_behind(piece, ("tm", "pol"), 1))
     turned = []
-    for k, (first, count) in enumerate(zip(starts, counts)):
-        spectra = filter_bank(samples, histories[k], coefficients, table, first, count, owners)
-        if k + 1 < len(counts):
-            spectra, histories[k + 1] = lax.optimization_barrier((spectra, histories[k + 1]))
+    for k in range(last + 1):
+        following = parts[k + 2] if k + 2 <= last else None
+        spectra, *pieces = filter_bank(
+            samples, histories[k], coefficients, table, starts[k], counts[k], owners, following
+        )
+        if following:
+            piece = pieces[0]
+            if k > 0:
+                piece, arrived = lax.optimization_barrier((piece, arrived))
+            piece, histories[k + 1] = lax.optimization_barrier((piece, histories[k + 1]))
+            histories.append(from_behind(piece, ("tm", "pol"), 1))
+        if k > 0:
+            turned.append(turn(arrived, sets, frames))
         arrived = lax.all_to_all(spectra, everyone, 0, 0, tiled=True)
-        turned.append(turn(arrived, sets, frames))
+    turned.append(turn(arrived, sets, frames))
     return correlate_all(turned, counts, sets, order, 1.0 / total_frames)
 
 

time: 295 us -> 276 us (0.936)
  waiting for transfers between devices: 132 us -> 111 us
  local copies, waits for them, and re-layouts: 14.8 us -> 7.28 us
  Pallas kernels: 100 us -> 106 us
  starting transfers between devices: 47.8 us -> 50.8 us
    ppermute x4, waiting for transfers between devices: 13.4 us -> 0.82 us  [from_behind(): return lax.ppermute(block, axis, route)]
    all_to_all x4, waiting for transfers between devices: 118 us -> 111 us  [fast(): arrived = lax.all_to_all(spectra, everyone, 0, 0, tiled=True)]
    pallas_call x4 -> x5, Pallas kernels: 70.7 us -> 77.5 us  [the longest x4 74.9 us: filter_bank(): pl.pallas_call(functools.partial(filter_bank_kernel, steps, following), o...]
    slice x4 -> x1, local copies, waits for them, and re-layouts: 7.88 us -> 1.29 us  [fast(): histories = [from_behind(samples[:counts[0]], ('tm', 'pol'), 1)]]
    all_to_all x4, starting transfers between devices: 42.7 us -> 45.7 us  [fast(): arrived = lax.all_to_all(spectra, everyone, 0, 0, tiled=True)]
  transfers between devices with their start and end apart: 8 -> 8, of which waited for: 6 -> 5; matrix products, arithmetic and copies ran while one was open for 1% -> 0% of each run, Pallas kernels for 27% -> 31%
where the time goes in v3:
time: 276 us
  waiting for transfers between devices  111 us (40%)
  Pallas kernels  106 us (38%)
  starting transfers between devices  50.8 us (18%)
  local copies, waits for them, and re-layouts  7.28 us (3%)
    all_to_all x4, waiting for transfers between devices, fast(): arrived = lax.all_to_all(spectra, everyone, 0, 0, tiled=True)  111 us
    pallas_call x4, Pallas kernels, filter_bank(): pl.pallas_call(functools.partial(filter_bank_kernel, steps, following), o...  74.9 us
    all_to_all x4, starting transfers between devices, fast(): arrived = lax.all_to_all(spectra, everyone, 0, 0, tiled=True)  45.7 us
    pallas_call x1, Pallas kernels, correlate_all(): pl.pallas_call(functools.partial(correlate_kernel, counts, sets, scale),...  17.6 us
    pallas_call x4, Pallas kernels, turn(): pl.pallas_call(functools.partial(turn_kernel, frames), out_shape=jax.Shap...  10.7 us
    unnamed x18, local copies, waits for them, and re-layouts  5.99 us
  transfers between devices with their start and end apart: 8, of which 5 were waited for; matrix products, arithmetic and copies ran while one was open for 0% of the time, Pallas kernels for 31%

profile of v3, /device:TPU:15, one launch (start us, length us, event | category | flops | bytes accessed | tf_op | source)
XLA Modules:
  0.0 275.6 jit_solution(7420716441356148649)
XLA Ops:
  0.0 1.3 slice.3
  1.3 1.3 collective-permute-start
  2.6 2.6 cut.1
  5.2 0.8 collective-permute-done.history_hbm
  6.0 0.0 copy-start.8
  6.0 1.3 collective-permute-start.1
  7.3 0.0 copy-done.8
  7.3 11.0 %filter_bank.4 = (bf16[16,128,256]{2,1,0:T(8,128)(2,1)}, bf16[16,16,4096]{2,1,0:T(8,128)(2,1)}) custom-call(bf16[64,16,4096]{2,1,0:T(8,128)(2,1)} %own_ref.7, f32[16,4096]{1,0:T(8,128)} %coef_ref.7, bf16[8,2,512,512]{3,2,1,0:T(8,128)(2,1)} %constant.65.clone.table_hbm, bf16[8,16,4096]{2,1,0:T(8,128)(2,1)} %copy-done.8, bf16[64,16,4096]{2,1,0:T(8,128)(2,1)} %own_ref.7), custom_call_target="tpu_custom_call" | custom-call | flops 99999997952 | bytes 16777216 | tf_op jit(solution)/shard_map/filter_bank/pallas_call | solution.py:308
  18.3 18.9 %all-to-all-start = ((bf16[16,128,256]{2,1,0:T(8,128)(2,1)}), bf16[16,128,256]{2,1,0:T(8,128)(2,1)S(1)}, u32[]{:S(2)}, u32[]{:S(2)}) async-start(bf16[16,128,256]{2,1,0:T(8,128)(2,1)} %get-tuple-element.22), calls=%async_computation | async-start | bytes 2097152 | tf_op jit(solution)/shard_map/all_to_all | solution.py:472
  37.2 0.0 collective-permute-done.1.history_hbm
  37.2 1.3 collective-permute-start.2
  38.5 18.8 %filter_bank.5 = (bf16[16,256,256]{2,1,0:T(8,128)(2,1)}, bf16[24,16,4096]{2,1,0:T(8,128)(2,1)}) custom-call(bf16[64,16,4096]{2,1,0:T(8,128)(2,1)} %own_ref.7, f32[16,4096]{1,0:T(8,128)} %coef_ref.7, bf16[8,2,512,512]{3,2,1,0:T(8,128)(2,1)} %constant.65.clone.table_hbm, bf16[16,16,4096]{2,1,0:T(8,128)(2,1)} %collective-permute-done.1.history_hbm, ...), custom_call_target="tpu_custom_call" | custom-call | flops 99999997952 | bytes 16777216 | tf_op jit(solution)/shard_map/filter_bank/pallas_call | solution.py:308
  57.2 5.2 %all-to-all-done.in_ref = bf16[16,128,256]{2,1,0:T(8,128)(2,1)S(1)} async-done(((bf16[16,128,256]{2,1,0:T(8,128)(2,1)}), bf16[16,128,256]{2,1,0:T(8,128)(2,1)S(1)}, u32[]{:S(2)}, u32[]{:S(2)}) %all-to-all-start) | async-done | bytes 1048608 | tf_op jit(solution)/shard_map/all_to_all | solution.py:472
  62.4 0.0 copy-start.6
  62.4 1.0 copy-done.6
  63.4 17.0 %all-to-all-start.1 = ((bf16[16,256,256]{2,1,0:T(8,128)(2,1)}), bf16[16,256,256]{2,1,0:T(8,128)(2,1)}, u32[]{:S(2)}, u32[]{:S(2)}) async-start(bf16[16,256,256]{2,1,0:T(8,128)(2,1)} %get-tuple-element.24), calls=%async_computation.1 | async-start | bytes 4194304 | tf_op jit(solution)/shard_map/all_to_all | solution.py:472
  80.4 0.0 collective-permute-done.2.history_hbm
  80.4 1.3 collective-permute-start.3
  81.7 18.7 %filter_bank.6 = bf16[16,256,256]{2,1,0:T(8,128)(2,1)} custom-call(bf16[64,16,4096]{2,1,0:T(8,128)(2,1)} %own_ref.7, f32[16,4096]{1,0:T(8,128)} %coef_ref.7, bf16[8,2,512,512]{3,2,1,0:T(8,128)(2,1)} %constant.65.clone.table_hbm, bf16[16,16,4096]{2,1,0:T(8,128)(2,1)} %collective-permute-done.2.history_hbm), custom_call_target="tpu_custom_call" | custom-call | flops 99999997952 | bytes 16777216 | tf_op jit(solution)/shard_map/filter_bank/pallas_call | solution.py:308
  100.4 27.8 %all-to-all-done.1.in_ref = bf16[16,256,256]{2,1,0:T(8,128)(2,1)} async-done(((bf16[16,256,256]{2,1,0:T(8,128)(2,1)}), bf16[16,256,256]{2,1,0:T(8,128)(2,1)}, u32[]{:S(2)}, u32[]{:S(2)}) %all-to-all-start.1) | async-done | bytes 2097184 | tf_op jit(solution)/shard_map/all_to_all | solution.py:472
  128.2 4.9 %all-to-all-start.2 = ((bf16[16,256,256]{2,1,0:T(8,128)(2,1)}), bf16[16,256,256]{2,1,0:T(8,128)(2,1)}, u32[]{:S(2)}, u32[]{:S(2)}) async-start(bf16[16,256,256]{2,1,0:T(8,128)(2,1)} %filter_bank.6), calls=%async_computation.2 | async-start | bytes 4194304 | tf_op jit(solution)/shard_map/all_to_all | solution.py:472
  133.1 0.0 collective-permute-done.3.history_hbm
  133.1 26.4 %filter_bank.7 = bf16[16,384,256]{2,1,0:T(8,128)(2,1)} custom-call(bf16[64,16,4096]{2,1,0:T(8,128)(2,1)} %own_ref.7, f32[16,4096]{1,0:T(8,128)} %coef_ref.7, bf16[8,2,512,512]{3,2,1,0:T(8,128)(2,1)} %constant.65.clone.table_hbm, bf16[24,16,4096]{2,1,0:T(8,128)(2,1)} %collective-permute-done.3.history_hbm), custom_call_target="tpu_custom_call" | custom-call | flops 99999997952 | bytes 16777216 | tf_op jit(solution)/shard_map/filter_bank/pallas_call | solution.py:308
  159.5 21.1 %all-to-all-done.2.in_ref = bf16[16,256,256]{2,1,0:T(8,128)(2,1)} async-done(((bf16[16,256,256]{2,1,0:T(8,128)(2,1)}), bf16[16,256,256]{2,1,0:T(8,128)(2,1)}, u32[]{:S(2)}, u32[]{:S(2)}) %all-to-all-start.2) | async-done | bytes 2097184 | tf_op jit(solution)/shard_map/all_to_all | solution.py:472
  180.6 5.0 %all-to-all-start.3 = ((bf16[16,384,256]{2,1,0:T(8,128)(2,1)}), bf16[16,384,256]{2,1,0:T(8,128)(2,1)S(1)}, u32[]{:S(2)}, u32[]{:S(2)}) async-start(bf16[16,384,256]{2,1,0:T(8,128)(2,1)} %filter_bank.7), calls=%async_computation.3 | async-start | bytes 6291456 | tf_op jit(solution)/shard_map/all_to_all | solution.py:472
  185.6 0.0 copy-start.7
  185.6 1.2 copy-done.7
  186.8 0.9 turn.4.refs_0_
  187.7 0.0 copy-start.4
  187.7 1.0 copy-done.4
  188.8 3.8 %turn.5.refs_1_ = bf16[128,64,128]{2,1,0:T(8,128)(2,1)S(1)} custom-call(bf16[16,256,256]{2,1,0:T(8,128)(2,1)} %all-to-all-done.1.in_ref), custom_call_target="tpu_custom_call" | custom-call | flops 4194304 | bytes 4194304 | tf_op jit(solution)/shard_map/turn/pallas_call | solution.py:371
  192.5 0.0 copy-start
  192.6 1.3 copy-done
  193.9 3.8 %turn.6.refs_2_ = bf16[128,64,128]{2,1,0:T(8,128)(2,1)S(1)} custom-call(bf16[16,256,256]{2,1,0:T(8,128)(2,1)} %all-to-all-done.2.in_ref), custom_call_target="tpu_custom_call" | custom-call | flops 4194304 | bytes 4194304 | tf_op jit(solution)/shard_map/turn/pallas_call | solution.py:371
  197.6 0.0 copy-start.2
  197.6 1.3 copy-done.2
  198.9 56.5 %all-to-all-done.3.in_ref = bf16[16,384,256]{2,1,0:T(8,128)(2,1)S(1)} async-done(((bf16[16,384,256]{2,1,0:T(8,128)(2,1)}), bf16[16,384,256]{2,1,0:T(8,128)(2,1)S(1)}, u32[]{:S(2)}, u32[]{:S(2)}) %all-to-all-start.3) | async-done | bytes 3145760 | tf_op jit(solution)/shard_map/all_to_all | solution.py:472
  255.5 0.0 copy-start.1
  255.5 0.0 copy-start.3
  255.5 0.0 copy-start.5
  255.5 2.3 turn.7.refs_3_
  257.9 0.0 copy-done.1
  257.9 0.0 copy-done.3
  257.9 0.1 copy-done.5
  258.0 17.6 %correlate.1 = f32[8,16,256,256]{3,2,1,0:T(8,128)} custom-call(s32[16]{0:T(128)S(1)} %compare_select_fusion.3.order_ref, bf16[128,32,128]{2,1,0:T(8,128)(2,1)S(1)} %copy-done.5, bf16[128,64,128]{2,1,0:T(8,128)(2,1)S(1)} %copy-done.1, bf16[128,64,128]{2,1,0:T(8,128)(2,1)S(1)} %copy-done.3, bf16[128,96,128]{2,1,0:T(8,128)(2,1)S(1)} %turn.7.refs_3_), custom_call_target="tpu_custom_call" | custom-call | flops 4294967296 | bytes 41943040 | tf_op jit(solution)/shard_map/correlate/pallas_call | solution.py:417
  (1 shorter events, 0.0 us)
Async XLA Ops:
  1.3 4.7 %collective-permute-start = (bf16[8,16,4096]{2,1,0:T(8,128)(2,1)S(1)}, bf16[8,16,4096]{2,1,0:T(8,128)(2,1)S(1)}, u32[]{:S(2)}, u32[]{:S(2)}) collective-permute-start(bf16[8,16,4096]{2,1,0:T(8,128)(2,1)S(1)} %slice.3), channel_id=1, source_target_pairs={{0,1},{1,2},{2,3},{4,5},{5,6},{6,7},{8,9},{9,10},{10,11},{12,13},{... | collective-permute-start | bytes 3145736 | tf_op jit(solution)/shard_map/ppermute | solution.py:23
  6.0 1.3 copy-start.8
  6.0 31.1 %collective-permute-start.1 = (bf16[16,16,4096]{2,1,0:T(8,128)(2,1)}, bf16[16,16,4096]{2,1,0:T(8,128)(2,1)}, u32[]{:S(2)}, u32[]{:S(2)}) collective-permute-start(bf16[16,16,4096]{2,1,0:T(8,128)(2,1)} %cut.1), channel_id=1, source_target_pairs={{0,1},{1,2},{2,3},{4,5},{5,6},{6,7},{8,9},{9,10},{10,11},{12,13},{... | collective-permute-start | bytes 6291464 | tf_op jit(solution)/shard_map/ppermute | solution.py:23
  18.3 44.1 %all-to-all-start = ((bf16[16,128,256]{2,1,0:T(8,128)(2,1)}), bf16[16,128,256]{2,1,0:T(8,128)(2,1)S(1)}, u32[]{:S(2)}, u32[]{:S(2)}) async-start(bf16[16,128,256]{2,1,0:T(8,128)(2,1)} %get-tuple-element.22), calls=%async_computation | async-start | bytes 2097152 | tf_op jit(solution)/shard_map/all_to_all | solution.py:472
  37.2 43.3 %collective-permute-start.2 = (bf16[16,16,4096]{2,1,0:T(8,128)(2,1)}, bf16[16,16,4096]{2,1,0:T(8,128)(2,1)}, u32[]{:S(2)}, u32[]{:S(2)}) collective-permute-start(bf16[16,16,4096]{2,1,0:T(8,128)(2,1)} %get-tuple-element.26), channel_id=1, source_target_pairs={{0,1},{1,2},{2,3},{4,5},{5,6},{6,7},{8,9},{9,10},{10,11},{12,13},{... | collective-permute-start | bytes 6291464 | tf_op jit(solution)/shard_map/ppermute | solution.py:23
  62.4 1.0 copy-start.6
  63.4 64.8 %all-to-all-start.1 = ((bf16[16,256,256]{2,1,0:T(8,128)(2,1)}), bf16[16,256,256]{2,1,0:T(8,128)(2,1)}, u32[]{:S(2)}, u32[]{:S(2)}) async-start(bf16[16,256,256]{2,1,0:T(8,128)(2,1)} %get-tuple-element.24), calls=%async_computation.1 | async-start | bytes 4194304 | tf_op jit(solution)/shard_map/all_to_all | solution.py:472
  80.4 52.7 %collective-permute-start.3 = (bf16[24,16,4096]{2,1,0:T(8,128)(2,1)}, bf16[24,16,4096]{2,1,0:T(8,128)(2,1)}, u32[]{:S(2)}, u32[]{:S(2)}) collective-permute-start(bf16[24,16,4096]{2,1,0:T(8,128)(2,1)} %get-tuple-element.28), channel_id=1, source_target_pairs={{0,1},{1,2},{2,3},{4,5},{5,6},{6,7},{8,9},{9,10},{10,11},{12,13},{... | collective-permute-start | bytes 9437192 | tf_op jit(solution)/shard_map/ppermute | solution.py:23
  128.2 52.4 %all-to-all-start.2 = ((bf16[16,256,256]{2,1,0:T(8,128)(2,1)}), bf16[16,256,256]{2,1,0:T(8,128)(2,1)}, u32[]{:S(2)}, u32[]{:S(2)}) async-start(bf16[16,256,256]{2,1,0:T(8,128)(2,1)} %filter_bank.6), calls=%async_computation.2 | async-start | bytes 4194304 | tf_op jit(solution)/shard_map/all_to_all | solution.py:472
  180.6 74.9 %all-to-all-start.3 = ((bf16[16,384,256]{2,1,0:T(8,128)(2,1)}), bf16[16,384,256]{2,1,0:T(8,128)(2,1)S(1)}, u32[]{:S(2)}, u32[]{:S(2)}) async-start(bf16[16,384,256]{2,1,0:T(8,128)(2,1)} %filter_bank.7), calls=%async_computation.3 | async-start | bytes 6291456 | tf_op jit(solution)/shard_map/all_to_all | solution.py:472
  185.6 1.2 copy-start.7
  187.7 1.1 copy-start.4
  192.5 1.3 copy-start
  197.6 1.3 copy-start.2
  255.5 2.4 copy-start.1
  255.5 2.4 copy-start.3
  255.5 2.5 copy-start.5

commit v4 on v3

--- a/solution.py
+++ b/solution.py
@@ -224,7 +224,7 @@
             kept_ref[block, pl.ds(f, inputs, stride=frames), :] = totals[f]
         return carry
 
-    lax.fori_loop(0, length // LANES, one_block, 0)
+    lax.fori_loop(0, length // LANES, one_block, 0, unroll=2)
     if following:
 
         @pl.when(step == 0)
@@ -248,7 +248,7 @@
                 low_ref[group, rows, lanes] = (pair[half] - top.astype(jnp.float32)).astype(jnp.bfloat16)
         return carry
 
-    lax.fori_loop(0, parts * inputs * frames // 16, one_rows, 0)
+    lax.fori_loop(0, parts * inputs * frames // 16, one_rows, 0, unroll=4)
 
     @pl.when(step == steps - 1)
     def _():
@@ -281,7 +281,7 @@
                         out_ref[block * slots + inside, pl.ds(first, 16), pl.ds(kind * LANES, LANES)] = now[inside].astype(jnp.bfloat16)
             return carry
 
-        lax.fori_loop(0, out_ref.shape[1] // 16, one_part, 0)
+        lax.fori_loop(0, out_ref.shape[1] // 16, one_part, 0, unroll=4)
         if following:
             store.wait()
 
@@ -360,7 +360,7 @@
         work_ref[pl.ds(i, LANES, stride=count), :] = square.T
         return carry
 
-    lax.fori_loop(0, count, one_input, 0, unroll=8)
+    lax.fori_loop(0, count, one_input, 0, unroll=count)
     out_ref[...] = work_ref[...].reshape(LANES, count, LANES).astype(jnp.bfloat16)
 
 
@@ -382,48 +382,74 @@
 
 
 def correlate_kernel(counts, sets, scale, order_ref, *refs):
-    *in_refs, out_ref = refs
-    held = out_ref.shape[0]
-
-    def one_channel(u, carry):
-        joined = jnp.concatenate(
-            [
-                in_ref[u, pl.ds(z * count, count), :]
-                for z in range(sets)
-                for in_ref, count in zip(in_refs, counts)
-            ],
-            axis=0,
-        )
-        turned = jnp.concatenate([joined[:, LANES // 2 :], -joined[:, : LANES // 2]], axis=1)
-        both = lax.dot_general(
-            jnp.concatenate([joined, turned], axis=0),
-            joined,
-            (((1,), (1,)), ((), ())),
-            preferred_element_type=jnp.float32,
-        )
-        real, imag = both[: joined.shape[0]], both[joined.shape[0] :]
-        row = lax.broadcasted_iota(jnp.int32, real.shape, 0)
-        col = lax.broadcasted_iota(jnp.int32, real.shape, 1)
-        out_ref[u, 0] = jnp.where(row <= col, real, imag) * scale
-        return carry
-
-    lax.fori_loop(0, held, one_channel, 0, unroll=held)
+    *in_refs, out_hbm, kept_ref, sems = refs
+    _, many, held, width, _ = kept_ref.shape
+    step = pl.program_id(0)
+    slot = step % 2
+
+    def copies(of_step, of_slot):
+        return [
+            pltpu.make_async_copy(
+                kept_ref.at[of_slot, k], out_hbm.at[:, order_ref[many * of_step + k]], sems.at[of_slot, k]
+            )
+            for k in range(many)
+        ]
+
+    @pl.when(step >= 2)
+    def _():
+        for copy in copies(step - 2, slot):
+            copy.wait()
+
+    row = lax.broadcasted_iota(jnp.int32, (width, width), 0)
+    col = lax.broadcasted_iota(jnp.int32, (width, width), 1)
+    for k in range(many):
+        for u in range(held):
+            joined = jnp.concatenate(
+                [
+                    in_ref[held * k + u, pl.ds(z * count, count), :]
+                    for z in range(sets)
+                    for in_ref, count in zip(in_refs, counts)
+                ],
+                axis=0,
+            )
+            turned = jnp.concatenate([joined[:, LANES // 2 :], -joined[:, : LANES // 2]], axis=1)
+            both = lax.dot_general(
+                jnp.concatenate([joined, turned], axis=0),
+                joined,
+                (((1,), (1,)), ((), ())),
+                preferred_element_type=jnp.float32,
+            )
+            kept_ref[slot, k, u] = jnp.where(row <= col, both[:width], both[width:]) * scale
+    for copy in copies(step, slot):
+        copy.start()
+
+    @pl.when(step == pl.num_programs(0) - 1)
+    def _():
+        for copy in copies(step - 1, 1 - slot) + copies(step, slot):
+            copy.wait()
 
 
 def correlate_all(turned, counts, sets, order, scale):
     channels = turned[0].shape[0]
     held = channels // RADIX
     width = sets * sum(counts)
+    many = 2
     out = pl.pallas_call(
         functools.partial(correlate_kernel, counts, sets, scale),
         out_shape=jax.ShapeDtypeStruct((held, RADIX, width, width), jnp.float32),
         grid_spec=pltpu.PrefetchScalarGridSpec(
             num_scalar_prefetch=1,
-            grid=(RADIX,),
-            in_specs=[pl.BlockSpec((held, sets * count, LANES), lambda s, order: (s, 0, 0)) for count in counts],
-            out_specs=pl.BlockSpec((held, 1, width, width), lambda s, order: (0, order[s], 0, 0)),
+            grid=(RADIX // many,),
+            in_specs=[
+                pl.BlockSpec((many * held, sets * count, LANES), lambda s, order: (s, 0, 0)) for count in counts
+            ],
+            out_specs=pl.BlockSpec(memory_space=pl.ANY),
+            scratch_shapes=[
+                pltpu.VMEM((2, many, held, width, width), jnp.float32),
+                pltpu.SemaphoreType.DMA((2, many)),
+            ],
         ),
-        compiler_params=pltpu.CompilerParams(vmem_limit_bytes=24 * MIB),
+        compiler_params=pltpu.CompilerParams(vmem_limit_bytes=36 * MIB),
         cost_estimate=pl.CostEstimate(
             flops=4 * channels * width * width * LANES, bytes_accessed=40 * MIB, transcendentals=0
         ),

time: 276 us -> 273 us (0.989)
  Pallas kernels: 106 us -> 97.4 us
  waiting for transfers between devices: 111 us -> 116 us
    pallas_call x4, Pallas kernels: 74.9 us -> 70.1 us  [filter_bank(): pl.pallas_call(functools.partial(filter_bank_kernel, steps, following), o...]
    all_to_all x4, waiting for transfers between devices: 111 us -> 115 us  [fast(): arrived = lax.all_to_all(spectra, everyone, 0, 0, tiled=True)]
  transfers between devices with their start and end apart: 8 -> 8, of which waited for: 5 -> 5; matrix products, arithmetic and copies ran while one was open for 0% -> 0% of each run, Pallas kernels for 31% -> 30%
where the time goes in v4:
time: 273 us; the launch traced here: 272 us
  waiting for transfers between devices  116 us (42%)
  Pallas kernels  97.4 us (36%)
  starting transfers between devices  50.4 us (18%)
  local copies, waits for them, and re-layouts  7.86 us (3%)
    all_to_all x4, waiting for transfers between devices, fast(): arrived = lax.all_to_all(spectra, everyone, 0, 0, tiled=True)  115 us
    pallas_call x4, Pallas kernels, filter_bank(): pl.pallas_call(functools.partial(filter_bank_kernel, steps, following), o...  70.1 us
    all_to_all x4, starting transfers between devices, fast(): arrived = lax.all_to_all(spectra, everyone, 0, 0, tiled=True)  45.3 us
    pallas_call x1, Pallas kernels, correlate_all(): pl.pallas_call(functools.partial(correlate_kernel, counts, sets, scale),...  14.9 us
    pallas_call x4, Pallas kernels, turn(): pl.pallas_call(functools.partial(turn_kernel, frames), out_shape=jax.Shap...  9.74 us
    unnamed x18, local copies, waits for them, and re-layouts  6.57 us
  transfers between devices with their start and end apart: 8, of which 5 were waited for; matrix products, arithmetic and copies ran while one was open for 0% of the time, Pallas kernels for 30%

profile of v4, /device:TPU:15, one launch (start us, length us, event | category | flops | bytes accessed | tf_op | source)
XLA Modules:
  0.0 272.0 jit_solution(14665904862465829892)
XLA Ops:
  0.0 1.3 slice.3
  1.3 1.3 collective-permute-start
  2.6 2.6 cut.1
  5.2 0.8 collective-permute-done.history_hbm
  6.0 0.0 copy-start.8
  6.0 1.3 collective-permute-start.1
  7.3 0.0 copy-done.8
  7.3 10.4 %filter_bank.4 = (bf16[16,128,256]{2,1,0:T(8,128)(2,1)}, bf16[16,16,4096]{2,1,0:T(8,128)(2,1)}) custom-call(bf16[64,16,4096]{2,1,0:T(8,128)(2,1)} %own_ref.7, f32[16,4096]{1,0:T(8,128)} %coef_ref.7, bf16[8,2,512,512]{3,2,1,0:T(8,128)(2,1)} %constant.65.clone.table_hbm, bf16[8,16,4096]{2,1,0:T(8,128)(2,1)} %copy-done.8, bf16[64,16,4096]{2,1,0:T(8,128)(2,1)} %own_ref.7), custom_call_target="tpu_custom_call" | custom-call | flops 99999997952 | bytes 16777216 | tf_op jit(solution)/shard_map/filter_bank/pallas_call | solution.py:308
  17.7 18.9 %all-to-all-start = ((bf16[16,128,256]{2,1,0:T(8,128)(2,1)}), bf16[16,128,256]{2,1,0:T(8,128)(2,1)S(1)}, u32[]{:S(2)}, u32[]{:S(2)}) async-start(bf16[16,128,256]{2,1,0:T(8,128)(2,1)} %get-tuple-element.22), calls=%async_computation | async-start | bytes 2097152 | tf_op jit(solution)/shard_map/all_to_all | solution.py:498
  36.6 0.0 collective-permute-done.1.history_hbm
  36.6 1.3 collective-permute-start.2
  37.9 17.6 %filter_bank.5 = (bf16[16,256,256]{2,1,0:T(8,128)(2,1)}, bf16[24,16,4096]{2,1,0:T(8,128)(2,1)}) custom-call(bf16[64,16,4096]{2,1,0:T(8,128)(2,1)} %own_ref.7, f32[16,4096]{1,0:T(8,128)} %coef_ref.7, bf16[8,2,512,512]{3,2,1,0:T(8,128)(2,1)} %constant.65.clone.table_hbm, bf16[16,16,4096]{2,1,0:T(8,128)(2,1)} %collective-permute-done.1.history_hbm, ...), custom_call_target="tpu_custom_call" | custom-call | flops 99999997952 | bytes 16777216 | tf_op jit(solution)/shard_map/filter_bank/pallas_call | solution.py:308
  55.5 6.4 %all-to-all-done.in_ref = bf16[16,128,256]{2,1,0:T(8,128)(2,1)S(1)} async-done(((bf16[16,128,256]{2,1,0:T(8,128)(2,1)}), bf16[16,128,256]{2,1,0:T(8,128)(2,1)S(1)}, u32[]{:S(2)}, u32[]{:S(2)}) %all-to-all-start) | async-done | bytes 1048608 | tf_op jit(solution)/shard_map/all_to_all | solution.py:498
  61.9 0.0 copy-start.6
  61.9 1.0 copy-done.6
  62.9 16.6 %all-to-all-start.1 = ((bf16[16,256,256]{2,1,0:T(8,128)(2,1)}), bf16[16,256,256]{2,1,0:T(8,128)(2,1)}, u32[]{:S(2)}, u32[]{:S(2)}) async-start(bf16[16,256,256]{2,1,0:T(8,128)(2,1)} %get-tuple-element.24), calls=%async_computation.1 | async-start | bytes 4194304 | tf_op jit(solution)/shard_map/all_to_all | solution.py:498
  79.5 0.0 collective-permute-done.2.history_hbm
  79.5 1.3 collective-permute-start.3
  80.8 17.5 %filter_bank.6 = bf16[16,256,256]{2,1,0:T(8,128)(2,1)} custom-call(bf16[64,16,4096]{2,1,0:T(8,128)(2,1)} %own_ref.7, f32[16,4096]{1,0:T(8,128)} %coef_ref.7, bf16[8,2,512,512]{3,2,1,0:T(8,128)(2,1)} %constant.65.clone.table_hbm, bf16[16,16,4096]{2,1,0:T(8,128)(2,1)} %collective-permute-done.2.history_hbm), custom_call_target="tpu_custom_call" | custom-call | flops 99999997952 | bytes 16777216 | tf_op jit(solution)/shard_map/filter_bank/pallas_call | solution.py:308
  98.3 29.0 %all-to-all-done.1.in_ref = bf16[16,256,256]{2,1,0:T(8,128)(2,1)} async-done(((bf16[16,256,256]{2,1,0:T(8,128)(2,1)}), bf16[16,256,256]{2,1,0:T(8,128)(2,1)}, u32[]{:S(2)}, u32[]{:S(2)}) %all-to-all-start.1) | async-done | bytes 2097184 | tf_op jit(solution)/shard_map/all_to_all | solution.py:498
  127.3 4.8 %all-to-all-start.2 = ((bf16[16,256,256]{2,1,0:T(8,128)(2,1)}), bf16[16,256,256]{2,1,0:T(8,128)(2,1)}, u32[]{:S(2)}, u32[]{:S(2)}) async-start(bf16[16,256,256]{2,1,0:T(8,128)(2,1)} %filter_bank.6), calls=%async_computation.2 | async-start | bytes 4194304 | tf_op jit(solution)/shard_map/all_to_all | solution.py:498
  132.1 0.0 collective-permute-done.3.history_hbm
  132.1 24.6 %filter_bank.7 = bf16[16,384,256]{2,1,0:T(8,128)(2,1)} custom-call(bf16[64,16,4096]{2,1,0:T(8,128)(2,1)} %own_ref.7, f32[16,4096]{1,0:T(8,128)} %coef_ref.7, bf16[8,2,512,512]{3,2,1,0:T(8,128)(2,1)} %constant.65.clone.table_hbm, bf16[24,16,4096]{2,1,0:T(8,128)(2,1)} %collective-permute-done.3.history_hbm), custom_call_target="tpu_custom_call" | custom-call | flops 99999997952 | bytes 16777216 | tf_op jit(solution)/shard_map/filter_bank/pallas_call | solution.py:308
  156.8 22.9 %all-to-all-done.2.in_ref = bf16[16,256,256]{2,1,0:T(8,128)(2,1)} async-done(((bf16[16,256,256]{2,1,0:T(8,128)(2,1)}), bf16[16,256,256]{2,1,0:T(8,128)(2,1)}, u32[]{:S(2)}, u32[]{:S(2)}) %all-to-all-start.2) | async-done | bytes 2097184 | tf_op jit(solution)/shard_map/all_to_all | solution.py:498
  179.7 5.0 %all-to-all-start.3 = ((bf16[16,384,256]{2,1,0:T(8,128)(2,1)}), bf16[16,384,256]{2,1,0:T(8,128)(2,1)S(1)}, u32[]{:S(2)}, u32[]{:S(2)}) async-start(bf16[16,384,256]{2,1,0:T(8,128)(2,1)} %filter_bank.7), calls=%async_computation.3 | async-start | bytes 6291456 | tf_op jit(solution)/shard_map/all_to_all | solution.py:498
  184.7 0.0 copy-start.7
  184.7 1.2 copy-done.7
  185.9 0.9 turn.4.refs_0_
  186.8 0.0 copy-start.4
  186.8 1.0 copy-done.4
  187.8 3.5 %turn.5.refs_1_ = bf16[128,64,128]{2,1,0:T(8,128)(2,1)S(1)} custom-call(bf16[16,256,256]{2,1,0:T(8,128)(2,1)} %all-to-all-done.1.in_ref), custom_call_target="tpu_custom_call" | custom-call | flops 4194304 | bytes 4194304 | tf_op jit(solution)/shard_map/turn/pallas_call | solution.py:371
  191.4 0.0 copy-start
  191.4 1.3 copy-done
  192.7 3.5 %turn.6.refs_2_ = bf16[128,64,128]{2,1,0:T(8,128)(2,1)S(1)} custom-call(bf16[16,256,256]{2,1,0:T(8,128)(2,1)} %all-to-all-done.2.in_ref), custom_call_target="tpu_custom_call" | custom-call | flops 4194304 | bytes 4194304 | tf_op jit(solution)/shard_map/turn/pallas_call | solution.py:371
  196.3 0.0 copy-start.2
  196.3 1.3 copy-done.2
  197.6 57.0 %all-to-all-done.3.in_ref = bf16[16,384,256]{2,1,0:T(8,128)(2,1)S(1)} async-done(((bf16[16,384,256]{2,1,0:T(8,128)(2,1)}), bf16[16,384,256]{2,1,0:T(8,128)(2,1)S(1)}, u32[]{:S(2)}, u32[]{:S(2)}) %all-to-all-start.3) | async-done | bytes 3145760 | tf_op jit(solution)/shard_map/all_to_all | solution.py:498
  254.5 0.0 copy-start.1
  254.5 0.0 copy-start.3
  254.5 0.0 copy-start.5
  254.5 1.8 turn.7.refs_3_
  256.3 0.0 copy-done.1
  256.3 0.4 copy-done.3
  256.8 0.3 copy-done.5
  257.0 14.9 %correlate.1 = f32[8,16,256,256]{3,2,1,0:T(8,128)} custom-call(s32[16]{0:T(128)S(1)} %compare_select_fusion.3.order_ref, bf16[128,32,128]{2,1,0:T(8,128)(2,1)S(1)} %copy-done.5, bf16[128,64,128]{2,1,0:T(8,128)(2,1)S(1)} %copy-done.1, bf16[128,64,128]{2,1,0:T(8,128)(2,1)S(1)} %copy-done.3, bf16[128,96,128]{2,1,0:T(8,128)(2,1)S(1)} %turn.7.refs_3_), custom_call_target="tpu_custom_call" | custom-call | flops 4294967296 | bytes 41943040 | tf_op jit(solution)/shard_map/correlate/pallas_call | solution.py:437
  (1 shorter events, 0.0 us)
Async XLA Ops:
  1.3 4.7 %collective-permute-start = (bf16[8,16,4096]{2,1,0:T(8,128)(2,1)S(1)}, bf16[8,16,4096]{2,1,0:T(8,128)(2,1)S(1)}, u32[]{:S(2)}, u32[]{:S(2)}) collective-permute-start(bf16[8,16,4096]{2,1,0:T(8,128)(2,1)S(1)} %slice.3), channel_id=1, source_target_pairs={{0,1},{1,2},{2,3},{4,5},{5,6},{6,7},{8,9},{9,10},{10,11},{12,13},{... | collective-permute-start | bytes 3145736 | tf_op jit(solution)/shard_map/ppermute | solution.py:23
  6.0 1.3 copy-start.8
  6.0 30.6 %collective-permute-start.1 = (bf16[16,16,4096]{2,1,0:T(8,128)(2,1)}, bf16[16,16,4096]{2,1,0:T(8,128)(2,1)}, u32[]{:S(2)}, u32[]{:S(2)}) collective-permute-start(bf16[16,16,4096]{2,1,0:T(8,128)(2,1)} %cut.1), channel_id=1, source_target_pairs={{0,1},{1,2},{2,3},{4,5},{5,6},{6,7},{8,9},{9,10},{10,11},{12,13},{... | collective-permute-start | bytes 6291464 | tf_op jit(solution)/shard_map/ppermute | solution.py:23
  17.7 44.1 %all-to-all-start = ((bf16[16,128,256]{2,1,0:T(8,128)(2,1)}), bf16[16,128,256]{2,1,0:T(8,128)(2,1)S(1)}, u32[]{:S(2)}, u32[]{:S(2)}) async-start(bf16[16,128,256]{2,1,0:T(8,128)(2,1)} %get-tuple-element.22), calls=%async_computation | async-start | bytes 2097152 | tf_op jit(solution)/shard_map/all_to_all | solution.py:498
  36.6 42.9 %collective-permute-start.2 = (bf16[16,16,4096]{2,1,0:T(8,128)(2,1)}, bf16[16,16,4096]{2,1,0:T(8,128)(2,1)}, u32[]{:S(2)}, u32[]{:S(2)}) collective-permute-start(bf16[16,16,4096]{2,1,0:T(8,128)(2,1)} %get-tuple-element.26), channel_id=1, source_target_pairs={{0,1},{1,2},{2,3},{4,5},{5,6},{6,7},{8,9},{9,10},{10,11},{12,13},{... | collective-permute-start | bytes 6291464 | tf_op jit(solution)/shard_map/ppermute | solution.py:23
  61.9 1.0 copy-start.6
  62.9 64.4 %all-to-all-start.1 = ((bf16[16,256,256]{2,1,0:T(8,128)(2,1)}), bf16[16,256,256]{2,1,0:T(8,128)(2,1)}, u32[]{:S(2)}, u32[]{:S(2)}) async-start(bf16[16,256,256]{2,1,0:T(8,128)(2,1)} %get-tuple-element.24), calls=%async_computation.1 | async-start | bytes 4194304 | tf_op jit(solution)/shard_map/all_to_all | solution.py:498
  79.5 52.7 %collective-permute-start.3 = (bf16[24,16,4096]{2,1,0:T(8,128)(2,1)}, bf16[24,16,4096]{2,1,0:T(8,128)(2,1)}, u32[]{:S(2)}, u32[]{:S(2)}) collective-permute-start(bf16[24,16,4096]{2,1,0:T(8,128)(2,1)} %get-tuple-element.28), channel_id=1, source_target_pairs={{0,1},{1,2},{2,3},{4,5},{5,6},{6,7},{8,9},{9,10},{10,11},{12,13},{... | collective-permute-start | bytes 9437192 | tf_op jit(solution)/shard_map/ppermute | solution.py:23
  127.3 52.3 %all-to-all-start.2 = ((bf16[16,256,256]{2,1,0:T(8,128)(2,1)}), bf16[16,256,256]{2,1,0:T(8,128)(2,1)}, u32[]{:S(2)}, u32[]{:S(2)}) async-start(bf16[16,256,256]{2,1,0:T(8,128)(2,1)} %filter_bank.6), calls=%async_computation.2 | async-start | bytes 4194304 | tf_op jit(solution)/shard_map/all_to_all | solution.py:498
  179.7 74.9 %all-to-all-start.3 = ((bf16[16,384,256]{2,1,0:T(8,128)(2,1)}), bf16[16,384,256]{2,1,0:T(8,128)(2,1)S(1)}, u32[]{:S(2)}, u32[]{:S(2)}) async-start(bf16[16,384,256]{2,1,0:T(8,128)(2,1)} %filter_bank.7), calls=%async_computation.3 | async-start | bytes 6291456 | tf_op jit(solution)/shard_map/all_to_all | solution.py:498
  184.7 1.2 copy-start.7
  186.8 1.1 copy-start.4
  191.4 1.3 copy-start
  196.3 1.3 copy-start.2
  254.5 1.8 copy-start.1
  254.5 2.2 copy-start.3
  254.5 2.5 copy-start.5

commit v5 on v4

--- a/solution.py
+++ b/solution.py
@@ -322,7 +322,7 @@
             pltpu.SemaphoreType.DMA((steps + 3,)),
         ]
         + ([pltpu.VMEM((following[1], frames, length), samples.dtype)] if following else []),
-        compiler_params=pltpu.CompilerParams(vmem_limit_bytes=62 * MIB),
+        compiler_params=pltpu.CompilerParams(vmem_limit_bytes=63 * MIB),
         cost_estimate=pl.CostEstimate(flops=10**11, bytes_accessed=16 * MIB, transcendentals=0),
         name="filter_bank",
     )(*operands)
@@ -433,7 +433,7 @@
     channels = turned[0].shape[0]
     held = channels // RADIX
     width = sets * sum(counts)
-    many = 2
+    many = 4
     out = pl.pallas_call(
         functools.partial(correlate_kernel, counts, sets, scale),
         out_shape=jax.ShapeDtypeStruct((held, RADIX, width, width), jnp.float32),

time: 273 us -> 272 us (level)
    unnamed x18 -> x14, local copies, waits for them, and re-layouts: 6.57 us -> 5.36 us
where the time goes in v5:
time: 272 us
  waiting for transfers between devices  116 us (43%)
  Pallas kernels  98.7 us (36%)
  starting transfers between devices  50.5 us (19%)
  local copies, waits for them, and re-layouts  6.65 us (2%)
    all_to_all x4, waiting for transfers between devices, fast(): arrived = lax.all_to_all(spectra, everyone, 0, 0, tiled=True)  115 us
    pallas_call x4, Pallas kernels, filter_bank(): pl.pallas_call(functools.partial(filter_bank_kernel, steps, following), o...  70.1 us
    all_to_all x4, starting transfers between devices, fast(): arrived = lax.all_to_all(spectra, everyone, 0, 0, tiled=True)  45.3 us
    pallas_call x1, Pallas kernels, correlate_all(): pl.pallas_call(functools.partial(correlate_kernel, counts, sets, scale),...  14.4 us
    pallas_call x4, Pallas kernels, turn(): pl.pallas_call(functools.partial(turn_kernel, frames), out_shape=jax.Shap...  11.5 us
  transfers between devices with their start and end apart: 8, of which 5 were waited for; matrix products, arithmetic and copies ran while one was open for 0% of the time, Pallas kernels for 30%

profile of v5, /device:TPU:15, one launch (start us, length us, event | category | flops | bytes accessed | tf_op | source)
XLA Modules:
  0.0 271.7 jit_solution(3077680574505139187)
XLA Ops:
  0.0 1.3 slice.3
  1.3 1.3 collective-permute-start
  2.6 2.6 cut.1
  5.2 0.8 collective-permute-done.history_hbm
  6.0 0.0 copy-start.6
  6.0 1.0 copy-done.6
  7.0 1.3 collective-permute-start.1
  8.3 10.4 %filter_bank.4 = (bf16[16,128,256]{2,1,0:T(8,128)(2,1)}, bf16[16,16,4096]{2,1,0:T(8,128)(2,1)}) custom-call(bf16[64,16,4096]{2,1,0:T(8,128)(2,1)} %own_ref.7, f32[16,4096]{1,0:T(8,128)} %coef_ref.7, bf16[8,2,512,512]{3,2,1,0:T(8,128)(2,1)} %constant.65.clone.table_hbm, bf16[8,16,4096]{2,1,0:T(8,128)(2,1)} %copy-done.6, bf16[64,16,4096]{2,1,0:T(8,128)(2,1)} %own_ref.7), custom_call_target="tpu_custom_call" | custom-call | flops 99999997952 | bytes 16777216 | tf_op jit(solution)/shard_map/filter_bank/pallas_call | solution.py:308
  18.7 18.9 %all-to-all-start = ((bf16[16,128,256]{2,1,0:T(8,128)(2,1)}), bf16[16,128,256]{2,1,0:T(8,128)(2,1)}, u32[]{:S(2)}, u32[]{:S(2)}) async-start(bf16[16,128,256]{2,1,0:T(8,128)(2,1)} %get-tuple-element.22), calls=%async_computation | async-start | bytes 2097152 | tf_op jit(solution)/shard_map/all_to_all | solution.py:498
  37.6 0.0 collective-permute-done.1.history_hbm
  37.6 1.3 collective-permute-start.2
  38.9 17.6 %filter_bank.5 = (bf16[16,256,256]{2,1,0:T(8,128)(2,1)}, bf16[24,16,4096]{2,1,0:T(8,128)(2,1)}) custom-call(bf16[64,16,4096]{2,1,0:T(8,128)(2,1)} %own_ref.7, f32[16,4096]{1,0:T(8,128)} %coef_ref.7, bf16[8,2,512,512]{3,2,1,0:T(8,128)(2,1)} %constant.65.clone.table_hbm, bf16[16,16,4096]{2,1,0:T(8,128)(2,1)} %collective-permute-done.1.history_hbm, ...), custom_call_target="tpu_custom_call" | custom-call | flops 99999997952 | bytes 16777216 | tf_op jit(solution)/shard_map/filter_bank/pallas_call | solution.py:308
  56.5 6.4 %all-to-all-done.in_ref = bf16[16,128,256]{2,1,0:T(8,128)(2,1)} async-done(((bf16[16,128,256]{2,1,0:T(8,128)(2,1)}), bf16[16,128,256]{2,1,0:T(8,128)(2,1)}, u32[]{:S(2)}, u32[]{:S(2)}) %all-to-all-start) | async-done | bytes 1048608 | tf_op jit(solution)/shard_map/all_to_all | solution.py:498
  62.9 16.7 %all-to-all-start.1 = ((bf16[16,256,256]{2,1,0:T(8,128)(2,1)}), bf16[16,256,256]{2,1,0:T(8,128)(2,1)}, u32[]{:S(2)}, u32[]{:S(2)}) async-start(bf16[16,256,256]{2,1,0:T(8,128)(2,1)} %get-tuple-element.24), calls=%async_computation.1 | async-start | bytes 4194304 | tf_op jit(solution)/shard_map/all_to_all | solution.py:498
  79.5 0.0 collective-permute-done.2.history_hbm
  79.5 1.3 collective-permute-start.3
  80.8 17.5 %filter_bank.6 = bf16[16,256,256]{2,1,0:T(8,128)(2,1)} custom-call(bf16[64,16,4096]{2,1,0:T(8,128)(2,1)} %own_ref.7, f32[16,4096]{1,0:T(8,128)} %coef_ref.7, bf16[8,2,512,512]{3,2,1,0:T(8,128)(2,1)} %constant.65.clone.table_hbm, bf16[16,16,4096]{2,1,0:T(8,128)(2,1)} %collective-permute-done.2.history_hbm), custom_call_target="tpu_custom_call" | custom-call | flops 99999997952 | bytes 16777216 | tf_op jit(solution)/shard_map/filter_bank/pallas_call | solution.py:308
  98.4 29.0 %all-to-all-done.1.in_ref = bf16[16,256,256]{2,1,0:T(8,128)(2,1)} async-done(((bf16[16,256,256]{2,1,0:T(8,128)(2,1)}), bf16[16,256,256]{2,1,0:T(8,128)(2,1)}, u32[]{:S(2)}, u32[]{:S(2)}) %all-to-all-start.1) | async-done | bytes 2097184 | tf_op jit(solution)/shard_map/all_to_all | solution.py:498
  127.3 4.8 %all-to-all-start.2 = ((bf16[16,256,256]{2,1,0:T(8,128)(2,1)}), bf16[16,256,256]{2,1,0:T(8,128)(2,1)}, u32[]{:S(2)}, u32[]{:S(2)}) async-start(bf16[16,256,256]{2,1,0:T(8,128)(2,1)} %filter_bank.6), calls=%async_computation.2 | async-start | bytes 4194304 | tf_op jit(solution)/shard_map/all_to_all | solution.py:498
  132.2 0.0 collective-permute-done.3.history_hbm
  132.2 24.6 %filter_bank.7 = bf16[16,384,256]{2,1,0:T(8,128)(2,1)} custom-call(bf16[64,16,4096]{2,1,0:T(8,128)(2,1)} %own_ref.7, f32[16,4096]{1,0:T(8,128)} %coef_ref.7, bf16[8,2,512,512]{3,2,1,0:T(8,128)(2,1)} %constant.65.clone.table_hbm, bf16[24,16,4096]{2,1,0:T(8,128)(2,1)} %collective-permute-done.3.history_hbm), custom_call_target="tpu_custom_call" | custom-call | flops 99999997952 | bytes 16777216 | tf_op jit(solution)/shard_map/filter_bank/pallas_call | solution.py:308
  156.8 22.9 %all-to-all-done.2.in_ref = bf16[16,256,256]{2,1,0:T(8,128)(2,1)} async-done(((bf16[16,256,256]{2,1,0:T(8,128)(2,1)}), bf16[16,256,256]{2,1,0:T(8,128)(2,1)}, u32[]{:S(2)}, u32[]{:S(2)}) %all-to-all-start.2) | async-done | bytes 2097184 | tf_op jit(solution)/shard_map/all_to_all | solution.py:498
  179.7 5.0 %all-to-all-start.3 = ((bf16[16,384,256]{2,1,0:T(8,128)(2,1)}), bf16[16,384,256]{2,1,0:T(8,128)(2,1)S(1)}, u32[]{:S(2)}, u32[]{:S(2)}) async-start(bf16[16,384,256]{2,1,0:T(8,128)(2,1)} %filter_bank.7), calls=%async_computation.3 | async-start | bytes 6291456 | tf_op jit(solution)/shard_map/all_to_all | solution.py:498
  184.7 2.6 turn.4.refs_0_
  187.3 0.0 copy-start.4
  187.3 1.0 copy-done.4
  188.3 3.5 %turn.5.refs_1_ = bf16[128,64,128]{2,1,0:T(8,128)(2,1)S(1)} custom-call(bf16[16,256,256]{2,1,0:T(8,128)(2,1)} %all-to-all-done.1.in_ref), custom_call_target="tpu_custom_call" | custom-call | flops 4194304 | bytes 4194304 | tf_op jit(solution)/shard_map/turn/pallas_call | solution.py:371
  191.9 0.0 copy-start
  191.9 1.3 copy-done
  193.2 3.5 %turn.6.refs_2_ = bf16[128,64,128]{2,1,0:T(8,128)(2,1)S(1)} custom-call(bf16[16,256,256]{2,1,0:T(8,128)(2,1)} %all-to-all-done.2.in_ref), custom_call_target="tpu_custom_call" | custom-call | flops 4194304 | bytes 4194304 | tf_op jit(solution)/shard_map/turn/pallas_call | solution.py:371
  196.8 0.0 copy-start.2
  196.8 1.3 copy-done.2
  198.1 56.5 %all-to-all-done.3.in_ref = bf16[16,384,256]{2,1,0:T(8,128)(2,1)S(1)} async-done(((bf16[16,384,256]{2,1,0:T(8,128)(2,1)}), bf16[16,384,256]{2,1,0:T(8,128)(2,1)S(1)}, u32[]{:S(2)}, u32[]{:S(2)}) %all-to-all-start.3) | async-done | bytes 3145760 | tf_op jit(solution)/shard_map/all_to_all | solution.py:498
  254.6 0.0 copy-start.1
  254.6 0.0 copy-start.3
  254.6 0.0 copy-start.5
  254.6 1.8 turn.7.refs_3_
  256.4 0.0 copy-done.1
  256.4 0.4 copy-done.3
  256.8 0.3 copy-done.5
  257.0 14.4 %correlate.1 = f32[8,16,256,256]{3,2,1,0:T(8,128)} custom-call(s32[16]{0:T(128)S(1)} %compare_select_fusion.3.order_ref, bf16[128,32,128]{2,1,0:T(8,128)(2,1)S(1)} %copy-done.5, bf16[128,64,128]{2,1,0:T(8,128)(2,1)S(1)} %copy-done.1, bf16[128,64,128]{2,1,0:T(8,128)(2,1)S(1)} %copy-done.3, bf16[128,96,128]{2,1,0:T(8,128)(2,1)S(1)} %turn.7.refs_3_), custom_call_target="tpu_custom_call" | custom-call | flops 4294967296 | bytes 41943040 | tf_op jit(solution)/shard_map/correlate/pallas_call | solution.py:437
  (1 shorter events, 0.0 us)
Async XLA Ops:
  1.3 4.7 %collective-permute-start = (bf16[8,16,4096]{2,1,0:T(8,128)(2,1)S(1)}, bf16[8,16,4096]{2,1,0:T(8,128)(2,1)S(1)}, u32[]{:S(2)}, u32[]{:S(2)}) collective-permute-start(bf16[8,16,4096]{2,1,0:T(8,128)(2,1)S(1)} %slice.3), channel_id=1, source_target_pairs={{0,1},{1,2},{2,3},{4,5},{5,6},{6,7},{8,9},{9,10},{10,11},{12,13},{... | collective-permute-start | bytes 3145736 | tf_op jit(solution)/shard_map/ppermute | solution.py:23
  6.0 1.0 copy-start.6
  7.0 30.5 %collective-permute-start.1 = (bf16[16,16,4096]{2,1,0:T(8,128)(2,1)}, bf16[16,16,4096]{2,1,0:T(8,128)(2,1)}, u32[]{:S(2)}, u32[]{:S(2)}) collective-permute-start(bf16[16,16,4096]{2,1,0:T(8,128)(2,1)} %cut.1), channel_id=1, source_target_pairs={{0,1},{1,2},{2,3},{4,5},{5,6},{6,7},{8,9},{9,10},{10,11},{12,13},{... | collective-permute-start | bytes 6291464 | tf_op jit(solution)/shard_map/ppermute | solution.py:23
  18.7 44.1 %all-to-all-start = ((bf16[16,128,256]{2,1,0:T(8,128)(2,1)}), bf16[16,128,256]{2,1,0:T(8,128)(2,1)}, u32[]{:S(2)}, u32[]{:S(2)}) async-start(bf16[16,128,256]{2,1,0:T(8,128)(2,1)} %get-tuple-element.22), calls=%async_computation | async-start | bytes 2097152 | tf_op jit(solution)/shard_map/all_to_all | solution.py:498
  37.6 41.9 %collective-permute-start.2 = (bf16[16,16,4096]{2,1,0:T(8,128)(2,1)}, bf16[16,16,4096]{2,1,0:T(8,128)(2,1)}, u32[]{:S(2)}, u32[]{:S(2)}) collective-permute-start(bf16[16,16,4096]{2,1,0:T(8,128)(2,1)} %get-tuple-element.26), channel_id=1, source_target_pairs={{0,1},{1,2},{2,3},{4,5},{5,6},{6,7},{8,9},{9,10},{10,11},{12,13},{... | collective-permute-start | bytes 6291464 | tf_op jit(solution)/shard_map/ppermute | solution.py:23
  62.9 64.5 %all-to-all-start.1 = ((bf16[16,256,256]{2,1,0:T(8,128)(2,1)}), bf16[16,256,256]{2,1,0:T(8,128)(2,1)}, u32[]{:S(2)}, u32[]{:S(2)}) async-start(bf16[16,256,256]{2,1,0:T(8,128)(2,1)} %get-tuple-element.24), calls=%async_computation.1 | async-start | bytes 4194304 | tf_op jit(solution)/shard_map/all_to_all | solution.py:498
  79.5 52.7 %collective-permute-start.3 = (bf16[24,16,4096]{2,1,0:T(8,128)(2,1)}, bf16[24,16,4096]{2,1,0:T(8,128)(2,1)}, u32[]{:S(2)}, u32[]{:S(2)}) collective-permute-start(bf16[24,16,4096]{2,1,0:T(8,128)(2,1)} %get-tuple-element.28), channel_id=1, source_target_pairs={{0,1},{1,2},{2,3},{4,5},{5,6},{6,7},{8,9},{9,10},{10,11},{12,13},{... | collective-permute-start | bytes 9437192 | tf_op jit(solution)/shard_map/ppermute | solution.py:23
  127.3 52.3 %all-to-all-start.2 = ((bf16[16,256,256]{2,1,0:T(8,128)(2,1)}), bf16[16,256,256]{2,1,0:T(8,128)(2,1)}, u32[]{:S(2)}, u32[]{:S(2)}) async-start(bf16[16,256,256]{2,1,0:T(8,128)(2,1)} %filter_bank.6), calls=%async_computation.2 | async-start | bytes 4194304 | tf_op jit(solution)/shard_map/all_to_all | solution.py:498
  179.7 74.9 %all-to-all-start.3 = ((bf16[16,384,256]{2,1,0:T(8,128)(2,1)}), bf16[16,384,256]{2,1,0:T(8,128)(2,1)S(1)}, u32[]{:S(2)}, u32[]{:S(2)}) async-start(bf16[16,384,256]{2,1,0:T(8,128)(2,1)} %filter_bank.7), calls=%async_computation.3 | async-start | bytes 6291456 | tf_op jit(solution)/shard_map/all_to_all | solution.py:498
  187.3 1.0 copy-start.4
  191.9 1.3 copy-start
  196.8 1.3 copy-start.2
  254.6 1.8 copy-start.1
  254.6 2.2 copy-start.3
  254.6 2.5 copy-start.5

commit v6 on v5

--- a/solution.py
+++ b/solution.py
@@ -224,7 +224,7 @@
             kept_ref[block, pl.ds(f, inputs, stride=frames), :] = totals[f]
         return carry
 
-    lax.fori_loop(0, length // LANES, one_block, 0, unroll=2)
+    lax.fori_loop(0, length // LANES, one_block, 0, unroll=4)
     if following:
 
         @pl.when(step == 0)
@@ -248,7 +248,7 @@
                 low_ref[group, rows, lanes] = (pair[half] - top.astype(jnp.float32)).astype(jnp.bfloat16)
         return carry
 
-    lax.fori_loop(0, parts * inputs * frames // 16, one_rows, 0, unroll=4)
+    lax.fori_loop(0, parts * inputs * frames // 16, one_rows, 0, unroll=8)
 
     @pl.when(step == steps - 1)
     def _():

time: 272 us -> 272 us (level)
  no operation moved by 1% of the time
where the time goes in v6:
time: 272 us
  waiting for transfers between devices  116 us (43%)
  Pallas kernels  98.1 us (36%)
  starting transfers between devices  50.4 us (19%)
  local copies, waits for them, and re-layouts  6.65 us (2%)
    all_to_all x4, waiting for transfers between devices, fast(): arrived = lax.all_to_all(spectra, everyone, 0, 0, tiled=True)  115 us
    pallas_call x4, Pallas kernels, filter_bank(): pl.pallas_call(functools.partial(filter_bank_kernel, steps, following), o...  69.5 us
    all_to_all x4, starting transfers between devices, fast(): arrived = lax.all_to_all(spectra, everyone, 0, 0, tiled=True)  45.2 us
    pallas_call x1, Pallas kernels, correlate_all(): pl.pallas_call(functools.partial(correlate_kernel, counts, sets, scale),...  14.4 us
    pallas_call x4, Pallas kernels, turn(): pl.pallas_call(functools.partial(turn_kernel, frames), out_shape=jax.Shap...  11.5 us
  transfers between devices with their start and end apart: 8, of which 5 were waited for; matrix products, arithmetic and copies ran while one was open for 0% of the time, Pallas kernels for 30%

profile of v6, /device:TPU:15, one launch (start us, length us, event | category | flops | bytes accessed | tf_op | source)
XLA Modules:
  0.0 271.5 jit_solution(989767949861987081)
XLA Ops:
  0.0 1.3 slice.3
  1.3 1.3 collective-permute-start
  2.6 2.6 cut.1
  5.2 0.8 collective-permute-done.history_hbm
  6.0 0.0 copy-start.6
  6.0 1.0 copy-done.6
  7.0 1.3 collective-permute-start.1
  8.3 10.3 %filter_bank.4 = (bf16[16,128,256]{2,1,0:T(8,128)(2,1)}, bf16[16,16,4096]{2,1,0:T(8,128)(2,1)}) custom-call(bf16[64,16,4096]{2,1,0:T(8,128)(2,1)} %own_ref.7, f32[16,4096]{1,0:T(8,128)} %coef_ref.7, bf16[8,2,512,512]{3,2,1,0:T(8,128)(2,1)} %constant.65.clone.table_hbm, bf16[8,16,4096]{2,1,0:T(8,128)(2,1)} %copy-done.6, bf16[64,16,4096]{2,1,0:T(8,128)(2,1)} %own_ref.7), custom_call_target="tpu_custom_call" | custom-call | flops 99999997952 | bytes 16777216 | tf_op jit(solution)/shard_map/filter_bank/pallas_call | solution.py:308
  18.7 18.9 %all-to-all-start = ((bf16[16,128,256]{2,1,0:T(8,128)(2,1)}), bf16[16,128,256]{2,1,0:T(8,128)(2,1)}, u32[]{:S(2)}, u32[]{:S(2)}) async-start(bf16[16,128,256]{2,1,0:T(8,128)(2,1)} %get-tuple-element.22), calls=%async_computation | async-start | bytes 2097152 | tf_op jit(solution)/shard_map/all_to_all | solution.py:498
  37.5 0.0 collective-permute-done.1.history_hbm
  37.5 1.3 collective-permute-start.2
  38.8 17.4 %filter_bank.5 = (bf16[16,256,256]{2,1,0:T(8,128)(2,1)}, bf16[24,16,4096]{2,1,0:T(8,128)(2,1)}) custom-call(bf16[64,16,4096]{2,1,0:T(8,128)(2,1)} %own_ref.7, f32[16,4096]{1,0:T(8,128)} %coef_ref.7, bf16[8,2,512,512]{3,2,1,0:T(8,128)(2,1)} %constant.65.clone.table_hbm, bf16[16,16,4096]{2,1,0:T(8,128)(2,1)} %collective-permute-done.1.history_hbm, ...), custom_call_target="tpu_custom_call" | custom-call | flops 99999997952 | bytes 16777216 | tf_op jit(solution)/shard_map/filter_bank/pallas_call | solution.py:308
  56.3 6.5 %all-to-all-done.in_ref = bf16[16,128,256]{2,1,0:T(8,128)(2,1)} async-done(((bf16[16,128,256]{2,1,0:T(8,128)(2,1)}), bf16[16,128,256]{2,1,0:T(8,128)(2,1)}, u32[]{:S(2)}, u32[]{:S(2)}) %all-to-all-start) | async-done | bytes 1048608 | tf_op jit(solution)/shard_map/all_to_all | solution.py:498
  62.8 16.6 %all-to-all-start.1 = ((bf16[16,256,256]{2,1,0:T(8,128)(2,1)}), bf16[16,256,256]{2,1,0:T(8,128)(2,1)}, u32[]{:S(2)}, u32[]{:S(2)}) async-start(bf16[16,256,256]{2,1,0:T(8,128)(2,1)} %get-tuple-element.24), calls=%async_computation.1 | async-start | bytes 4194304 | tf_op jit(solution)/shard_map/all_to_all | solution.py:498
  79.4 0.0 collective-permute-done.2.history_hbm
  79.4 1.3 collective-permute-start.3
  80.7 17.4 %filter_bank.6 = bf16[16,256,256]{2,1,0:T(8,128)(2,1)} custom-call(bf16[64,16,4096]{2,1,0:T(8,128)(2,1)} %own_ref.7, f32[16,4096]{1,0:T(8,128)} %coef_ref.7, bf16[8,2,512,512]{3,2,1,0:T(8,128)(2,1)} %constant.65.clone.table_hbm, bf16[16,16,4096]{2,1,0:T(8,128)(2,1)} %collective-permute-done.2.history_hbm), custom_call_target="tpu_custom_call" | custom-call | flops 99999997952 | bytes 16777216 | tf_op jit(solution)/shard_map/filter_bank/pallas_call | solution.py:308
  98.1 29.1 %all-to-all-done.1.in_ref = bf16[16,256,256]{2,1,0:T(8,128)(2,1)} async-done(((bf16[16,256,256]{2,1,0:T(8,128)(2,1)}), bf16[16,256,256]{2,1,0:T(8,128)(2,1)}, u32[]{:S(2)}, u32[]{:S(2)}) %all-to-all-start.1) | async-done | bytes 2097184 | tf_op jit(solution)/shard_map/all_to_all | solution.py:498
  127.2 4.8 %all-to-all-start.2 = ((bf16[16,256,256]{2,1,0:T(8,128)(2,1)}), bf16[16,256,256]{2,1,0:T(8,128)(2,1)}, u32[]{:S(2)}, u32[]{:S(2)}) async-start(bf16[16,256,256]{2,1,0:T(8,128)(2,1)} %filter_bank.6), calls=%async_computation.2 | async-start | bytes 4194304 | tf_op jit(solution)/shard_map/all_to_all | solution.py:498
  132.0 0.0 collective-permute-done.3.history_hbm
  132.0 24.4 %filter_bank.7 = bf16[16,384,256]{2,1,0:T(8,128)(2,1)} custom-call(bf16[64,16,4096]{2,1,0:T(8,128)(2,1)} %own_ref.7, f32[16,4096]{1,0:T(8,128)} %coef_ref.7, bf16[8,2,512,512]{3,2,1,0:T(8,128)(2,1)} %constant.65.clone.table_hbm, bf16[24,16,4096]{2,1,0:T(8,128)(2,1)} %collective-permute-done.3.history_hbm), custom_call_target="tpu_custom_call" | custom-call | flops 99999997952 | bytes 16777216 | tf_op jit(solution)/shard_map/filter_bank/pallas_call | solution.py:308
  156.4 23.1 %all-to-all-done.2.in_ref = bf16[16,256,256]{2,1,0:T(8,128)(2,1)} async-done(((bf16[16,256,256]{2,1,0:T(8,128)(2,1)}), bf16[16,256,256]{2,1,0:T(8,128)(2,1)}, u32[]{:S(2)}, u32[]{:S(2)}) %all-to-all-start.2) | async-done | bytes 2097184 | tf_op jit(solution)/shard_map/all_to_all | solution.py:498
  179.5 5.0 %all-to-all-start.3 = ((bf16[16,384,256]{2,1,0:T(8,128)(2,1)}), bf16[16,384,256]{2,1,0:T(8,128)(2,1)S(1)}, u32[]{:S(2)}, u32[]{:S(2)}) async-start(bf16[16,384,256]{2,1,0:T(8,128)(2,1)} %filter_bank.7), calls=%async_computation.3 | async-start | bytes 6291456 | tf_op jit(solution)/shard_map/all_to_all | solution.py:498
  184.5 2.6 turn.4.refs_0_
  187.1 0.0 copy-start.4
  187.1 1.0 copy-done.4
  188.2 3.5 %turn.5.refs_1_ = bf16[128,64,128]{2,1,0:T(8,128)(2,1)S(1)} custom-call(bf16[16,256,256]{2,1,0:T(8,128)(2,1)} %all-to-all-done.1.in_ref), custom_call_target="tpu_custom_call" | custom-call | flops 4194304 | bytes 4194304 | tf_op jit(solution)/shard_map/turn/pallas_call | solution.py:371
  191.7 0.0 copy-start
  191.7 1.3 copy-done
  193.1 3.5 %turn.6.refs_2_ = bf16[128,64,128]{2,1,0:T(8,128)(2,1)S(1)} custom-call(bf16[16,256,256]{2,1,0:T(8,128)(2,1)} %all-to-all-done.2.in_ref), custom_call_target="tpu_custom_call" | custom-call | flops 4194304 | bytes 4194304 | tf_op jit(solution)/shard_map/turn/pallas_call | solution.py:371
  196.6 0.0 copy-start.2
  196.6 1.3 copy-done.2
  197.9 56.5 %all-to-all-done.3.in_ref = bf16[16,384,256]{2,1,0:T(8,128)(2,1)S(1)} async-done(((bf16[16,384,256]{2,1,0:T(8,128)(2,1)}), bf16[16,384,256]{2,1,0:T(8,128)(2,1)S(1)}, u32[]{:S(2)}, u32[]{:S(2)}) %all-to-all-start.3) | async-done | bytes 3145760 | tf_op jit(solution)/shard_map/all_to_all | solution.py:498
  254.4 0.0 copy-start.1
  254.4 0.0 copy-start.3
  254.4 0.0 copy-start.5
  254.4 1.8 turn.7.refs_3_
  256.2 0.0 copy-done.1
  256.2 0.4 copy-done.3
  256.6 0.3 copy-done.5
  256.9 14.4 %correlate.1 = f32[8,16,256,256]{3,2,1,0:T(8,128)} custom-call(s32[16]{0:T(128)S(1)} %compare_select_fusion.3.order_ref, bf16[128,32,128]{2,1,0:T(8,128)(2,1)S(1)} %copy-done.5, bf16[128,64,128]{2,1,0:T(8,128)(2,1)S(1)} %copy-done.1, bf16[128,64,128]{2,1,0:T(8,128)(2,1)S(1)} %copy-done.3, bf16[128,96,128]{2,1,0:T(8,128)(2,1)S(1)} %turn.7.refs_3_), custom_call_target="tpu_custom_call" | custom-call | flops 4294967296 | bytes 41943040 | tf_op jit(solution)/shard_map/correlate/pallas_call | solution.py:437
  (1 shorter events, 0.0 us)
Async XLA Ops:
  1.3 4.7 %collective-permute-start = (bf16[8,16,4096]{2,1,0:T(8,128)(2,1)S(1)}, bf16[8,16,4096]{2,1,0:T(8,128)(2,1)S(1)}, u32[]{:S(2)}, u32[]{:S(2)}) collective-permute-start(bf16[8,16,4096]{2,1,0:T(8,128)(2,1)S(1)} %slice.3), channel_id=1, source_target_pairs={{0,1},{1,2},{2,3},{4,5},{5,6},{6,7},{8,9},{9,10},{10,11},{12,13},{... | collective-permute-start | bytes 3145736 | tf_op jit(solution)/shard_map/ppermute | solution.py:23
  6.0 1.0 copy-start.6
  7.0 30.5 %collective-permute-start.1 = (bf16[16,16,4096]{2,1,0:T(8,128)(2,1)}, bf16[16,16,4096]{2,1,0:T(8,128)(2,1)}, u32[]{:S(2)}, u32[]{:S(2)}) collective-permute-start(bf16[16,16,4096]{2,1,0:T(8,128)(2,1)} %cut.1), channel_id=1, source_target_pairs={{0,1},{1,2},{2,3},{4,5},{5,6},{6,7},{8,9},{9,10},{10,11},{12,13},{... | collective-permute-start | bytes 6291464 | tf_op jit(solution)/shard_map/ppermute | solution.py:23
  18.7 44.1 %all-to-all-start = ((bf16[16,128,256]{2,1,0:T(8,128)(2,1)}), bf16[16,128,256]{2,1,0:T(8,128)(2,1)}, u32[]{:S(2)}, u32[]{:S(2)}) async-start(bf16[16,128,256]{2,1,0:T(8,128)(2,1)} %get-tuple-element.22), calls=%async_computation | async-start | bytes 2097152 | tf_op jit(solution)/shard_map/all_to_all | solution.py:498
  37.5 41.8 %collective-permute-start.2 = (bf16[16,16,4096]{2,1,0:T(8,128)(2,1)}, bf16[16,16,4096]{2,1,0:T(8,128)(2,1)}, u32[]{:S(2)}, u32[]{:S(2)}) collective-permute-start(bf16[16,16,4096]{2,1,0:T(8,128)(2,1)} %get-tuple-element.26), channel_id=1, source_target_pairs={{0,1},{1,2},{2,3},{4,5},{5,6},{6,7},{8,9},{9,10},{10,11},{12,13},{... | collective-permute-start | bytes 6291464 | tf_op jit(solution)/shard_map/ppermute | solution.py:23
  62.8 64.4 %all-to-all-start.1 = ((bf16[16,256,256]{2,1,0:T(8,128)(2,1)}), bf16[16,256,256]{2,1,0:T(8,128)(2,1)}, u32[]{:S(2)}, u32[]{:S(2)}) async-start(bf16[16,256,256]{2,1,0:T(8,128)(2,1)} %get-tuple-element.24), calls=%async_computation.1 | async-start | bytes 4194304 | tf_op jit(solution)/shard_map/all_to_all | solution.py:498
  79.4 52.7 %collective-permute-start.3 = (bf16[24,16,4096]{2,1,0:T(8,128)(2,1)}, bf16[24,16,4096]{2,1,0:T(8,128)(2,1)}, u32[]{:S(2)}, u32[]{:S(2)}) collective-permute-start(bf16[24,16,4096]{2,1,0:T(8,128)(2,1)} %get-tuple-element.28), channel_id=1, source_target_pairs={{0,1},{1,2},{2,3},{4,5},{5,6},{6,7},{8,9},{9,10},{10,11},{12,13},{... | collective-permute-start | bytes 9437192 | tf_op jit(solution)/shard_map/ppermute | solution.py:23
  127.2 52.3 %all-to-all-start.2 = ((bf16[16,256,256]{2,1,0:T(8,128)(2,1)}), bf16[16,256,256]{2,1,0:T(8,128)(2,1)}, u32[]{:S(2)}, u32[]{:S(2)}) async-start(bf16[16,256,256]{2,1,0:T(8,128)(2,1)} %filter_bank.6), calls=%async_computation.2 | async-start | bytes 4194304 | tf_op jit(solution)/shard_map/all_to_all | solution.py:498
  179.5 74.9 %all-to-all-start.3 = ((bf16[16,384,256]{2,1,0:T(8,128)(2,1)}), bf16[16,384,256]{2,1,0:T(8,128)(2,1)S(1)}, u32[]{:S(2)}, u32[]{:S(2)}) async-start(bf16[16,384,256]{2,1,0:T(8,128)(2,1)} %filter_bank.7), calls=%async_computation.3 | async-start | bytes 6291456 | tf_op jit(solution)/shard_map/all_to_all | solution.py:498
  187.1 1.0 copy-start.4
  191.7 1.3 copy-start
  196.6 1.3 copy-start.2
  254.4 1.8 copy-start.1
  254.4 2.2 copy-start.3
  254.4 2.5 copy-start.5
